TPU v7x, 32 devices: a whole 2x2x4 slice. The times are simulated.
32 devices in a mesh: groups: 2 (over y), seq: 4 (over z), head: 2 (over x), section: 2 (over core).
Axes of the slice: x: 2, y: 2, z: 4, core: 2. Of those that a mesh axis runs over, the one named last changes fastest.
Arguments:
- q_heads: bfloat16 [2, 1024, 12288], P('section', ('groups', 'seq'), 'head'), parts along dimension 1, may hold values from -256 to 256
- cache_latent: bfloat16 [2, 1024, 512], P('section', ('groups', 'seq')), parts along dimension 1, may hold values from -6 to 6
- cache_rope: bfloat16 [2, 1024, 64], P('section', ('groups', 'seq')), parts along dimension 1, may hold values from -6.5 to 6.5
- span_start: int32 [2, 4], P('section', 'groups'), parts along dimension 1, may hold values from 1 to 256, as said below
- prefix_len: int32 [2, 4], P('section', 'groups'), parts along dimension 1, may hold values from 0 to 256, as said below
- key_up: bfloat16 [2, 64, 128, 512], P('section', 'head'), may hold values from -0.5 to 0.5
- value_up: bfloat16 [2, 64, 512, 128], P('section', 'head'), may hold values from -2 to 2
- out_weight: bfloat16 [2, 8192, 7168], P('section', 'head', 'seq'), may hold values from -0.0625 to 0.0625
Outputs:
- mixed_out: bfloat16 [2, 1024, 7168], P('section', ('groups', 'head'), 'seq'), parts along dimension 1
There are 2 independent parts, one for each index of `groups`. A program takes and returns all parts, laid end to end along the dimension named above; an argument that names none is the same for every part. Nothing has to cross between parts.
Inputs may be any that keep to these rules, and one draw needn't show every extreme that they name: Span j's own tokens are context positions span_start to span_start + 255; the last span of every layer starts at 256. `prefix_len`: below the span's span_start for every span but the last; equal to it for the last span of every layer.
All inputs are finite; a program needn't handle non-finite values.
Results may differ from a plain program's by a relative error of at most 0.0085.
Values may be sent and summed in bfloat16 or wider, within the bound.
No kernel may reach another device: no remote copies, remote signals or barrier semaphores. Data moves between devices by JAX's collectives and lax.ppermute only.
A program may use at most 64 MiB of HBM per device.

v0:
```python
import functools

import jax
import jax.numpy as jnp
from jax import lax
from jax.experimental import pallas as pl
from jax.experimental.pallas import tpu as pltpu
from jax.sharding import PartitionSpec as P


NSPAN = 2

SHARES = (2, 2, 2, 2)
CHUNKS = len(SHARES)
PREPARE_FLOPS = 10_000_000_000
EVERYWHERE_SHARE = 8
DIRECT = (False, False, False, False)

masked_fill = -1e30

VMEM = pl.BlockSpec(memory_space=pltpu.VMEM)
SMEM = pl.BlockSpec(memory_space=pltpu.SMEM)


def exchange(value, axis, distance):
    count = lax.axis_size(axis)
    return lax.ppermute(value, axis, [(i, i ^ distance) for i in range(count)])


def prepare_kernel(latent_ref, rope_ref, keys_ref, half_ref, loaded_ref, sems):
    lat_dim = latent_ref.shape[1]
    half = half_ref.shape[0]
    latent_copy = pltpu.make_async_copy(latent_ref, keys_ref.at[:, :lat_dim], sems.at[0])
    rope_copy = pltpu.make_async_copy(rope_ref, loaded_ref, sems.at[1])
    latent_copy.start()
    rope_copy.start()
    rope_copy.wait()
    keys_ref[:, lat_dim:] = jnp.concatenate([loaded_ref[...]] * 2, axis=0).T
    latent_copy.wait()
    first = pl.multiple_of(lax.axis_index("head") * half, half)
    half_ref[...] = keys_ref[pl.ds(first, half), :]


def prepare(latent, rope):
    tokens, lat_dim = latent.shape
    rope_dim = rope.shape[0]
    width = lat_dim + 2 * rope_dim
    return pl.pallas_call(
        prepare_kernel,
        in_specs=[pl.BlockSpec(memory_space=pl.ANY)] * 2,
        out_specs=[VMEM] * 2,
        scratch_shapes=[
            pltpu.VMEM((rope_dim, tokens), rope.dtype),
            pltpu.SemaphoreType.DMA((2,)),
        ],
        out_shape=[
            jax.ShapeDtypeStruct((tokens, width), latent.dtype),
            jax.ShapeDtypeStruct((tokens // 2, width), latent.dtype),
        ],
        compiler_params=pltpu.CompilerParams(vmem_limit_bytes=2 << 20),
        cost_estimate=pl.CostEstimate(
            flops=PREPARE_FLOPS, bytes_accessed=4 * latent.size, transcendentals=0
        ),
    )(latent, rope)


def absorb_into(query_ref, key_up_ref, out_ref, first_head, nope_dim, rope_dim):
    heads, tokens, _ = out_ref.shape
    lat_dim = key_up_ref.shape[2]
    pair_width = 2 * (nope_dim + rope_dim)
    lane = lax.broadcasted_iota(jnp.int32, (tokens, 2 * rope_dim), 1)
    pad = jnp.zeros((rope_dim, lat_dim), key_up_ref.dtype)
    for head in range(0, heads, 2):
        base = head // 2 * pair_width
        even_nope = query_ref[:, base : base + nope_dim]
        even_rope = query_ref[:, base + nope_dim : base + nope_dim + 2 * rope_dim]
        odd_all = query_ref[:, base + nope_dim : base + pair_width]
        odd_rope = query_ref[:, base + pair_width - 2 * rope_dim : base + pair_width]
        odd_map = jnp.concatenate([pad, key_up_ref[first_head + head + 1], pad], axis=0)
        out_ref[head, :, :lat_dim] = jnp.dot(
            even_nope, key_up_ref[first_head + head], preferred_element_type=jnp.float32
        ).astype(out_ref.dtype)
        out_ref[head + 1, :, :lat_dim] = jnp.dot(
            odd_all, odd_map, preferred_element_type=jnp.float32
        ).astype(out_ref.dtype)
        zero = jnp.zeros_like(even_rope)
        out_ref[head, :, lat_dim:] = jnp.where(lane < rope_dim, even_rope, zero)
        out_ref[head + 1, :, lat_dim:] = jnp.where(lane >= rope_dim, odd_rope, zero)


def absorb(queries, key_up, rope_dim, heads):
    tokens = queries.shape[0]
    _, nope_dim, lat_dim = key_up.shape
    out_dim = lat_dim + 2 * rope_dim

    def kernel(query_ref, key_up_ref, out_ref):
        absorb_into(query_ref, key_up_ref, out_ref, 0, nope_dim, rope_dim)

    return pl.pallas_call(
        kernel,
        in_specs=[VMEM] * 2,
        out_specs=VMEM,
        out_shape=jax.ShapeDtypeStruct((heads, tokens, out_dim), queries.dtype),
        compiler_params=pltpu.CompilerParams(vmem_limit_bytes=12 << 20),
        cost_estimate=pl.CostEstimate(
            flops=2 * tokens * heads * nope_dim * lat_dim,
            bytes_accessed=2 * (queries.size + key_up.size + heads * tokens * out_dim),
            transcendentals=0,
        ),
    )(queries, key_up)


def load_keys(own_ref, mine_refs, other_refs, keys_ref, keys_t_ref):
    block = own_ref.shape[0]
    half = block // 2
    keys_ref[:block, :] = own_ref[...]
    mine = lax.axis_index("head") * half
    for slot in range(1, 4):
        first = pl.multiple_of(slot * block + mine, half)
        keys_ref[pl.ds(first, half), :] = mine_refs[slot - 1][...]
        first = pl.multiple_of(slot * block + half - mine, half)
        keys_ref[pl.ds(first, half), :] = other_refs[slot - 1][...]
    keys_t_ref[...] = keys_ref[...].T


def hide_of(start_ref, prefix_ref, slot, first_token, tokens, block, context):
    here = lax.axis_index("seq")
    there = lax.bitwise_xor(here, slot)
    span_blocks = context // block // NSPAN
    span_first = start_ref[there // span_blocks]
    prefix = prefix_ref[there // span_blocks]
    first_pos = span_first + there % span_blocks * block + first_token
    column = lax.broadcasted_iota(jnp.int32, (tokens, context), 1)
    row = lax.broadcasted_iota(jnp.int32, (tokens, context), 0)
    position = lax.bitwise_xor(column // block, here) * block + column % block
    visible = (position < prefix) | ((position >= span_first) & (position <= row + first_pos))
    return jnp.where(visible, 0.0, masked_fill)


def attention(query, keys_ref, keys_t_ref, hide, softmax_scale, lat_dim):
    heads, tokens, width = query.shape
    context = keys_ref.shape[0]
    scores = jnp.dot(
        query.reshape(heads * tokens, width), keys_t_ref[...], preferred_element_type=jnp.float32
    )
    scores = scores.reshape(heads, tokens, context) + hide[None]
    peak = jnp.max(scores, axis=2, keepdims=True)
    weights = jnp.exp((scores - peak) * softmax_scale)
    inverse = 1.0 / jnp.sum(weights, axis=2, keepdims=True)
    rounded = weights.astype(keys_ref.dtype).reshape(heads * tokens, context)
    summed = jnp.dot(rounded, keys_ref[:, :lat_dim], preferred_element_type=jnp.float32)
    return (summed.reshape(heads, tokens, lat_dim) * inverse).astype(keys_ref.dtype)


def attend_heads(
    start_ref, prefix_ref, query_ref, value_up_ref, keys_ref, keys_t_ref, out_ref,
    softmax_scale, first_token, head_block,
):
    heads, block, _ = query_ref.shape
    tokens = out_ref.shape[0]
    _, lat_dim, value_dim = value_up_ref.shape
    hide = hide_of(start_ref, prefix_ref, 0, first_token, tokens, block, keys_ref.shape[0])
    for base in range(0, heads, head_block):
        latent_out = attention(
            query_ref[base : base + head_block, first_token : first_token + tokens, :],
            keys_ref, keys_t_ref, hide, softmax_scale, lat_dim,
        )
        for head in range(head_block):
            out_ref[:, (base + head) * value_dim : (base + head + 1) * value_dim] = jnp.dot(
                latent_out[head], value_up_ref[base + head], preferred_element_type=jnp.float32
            ).astype(out_ref.dtype)


def attend_kernel(
    start_ref, prefix_ref, query_ref, value_up_ref, *refs, softmax_scale, first_token, head_block
):
    if len(refs) > 3:
        own_ref, *received, out_ref, keys_ref, keys_t_ref = refs
        load_keys(own_ref, received[:3], received[3:], keys_ref, keys_t_ref)
    else:
        keys_ref, keys_t_ref, out_ref = refs
    attend_heads(
        start_ref, prefix_ref, query_ref, value_up_ref, keys_ref, keys_t_ref, out_ref,
        softmax_scale, first_token, head_block,
    )


def attend(spans, absorbed, keys, value_up, softmax_scale, first_token, tokens, context):
    heads, _, width = absorbed.shape
    _, lat_dim, value_dim = value_up.shape
    out_shape = [jax.ShapeDtypeStruct((tokens, heads * value_dim), absorbed.dtype)]
    if len(keys) > 2:
        out_shape.append(jax.ShapeDtypeStruct((context, width), absorbed.dtype))
        out_shape.append(jax.ShapeDtypeStruct((width, context), absorbed.dtype))
    return pl.pallas_call(
        functools.partial(
            attend_kernel,
            softmax_scale=softmax_scale,
            first_token=first_token,
            head_block=heads // 2,
        ),
        in_specs=[SMEM] * 2 + [VMEM] * (2 + len(keys)),
        out_specs=[VMEM] * len(out_shape),
        out_shape=out_shape,
        compiler_params=pltpu.CompilerParams(vmem_limit_bytes=24 << 20),
        cost_estimate=pl.CostEstimate(
            flops=2 * tokens * heads * (context * (width + lat_dim) + lat_dim * value_dim),
            bytes_accessed=2 * (heads * tokens * width + value_up.size + heads * tokens * value_dim),
            transcendentals=heads * tokens * context,
        ),
    )(*spans, absorbed, value_up, *keys)


def everywhere_kernel(
    start_ref, prefix_ref, query0_ref, query1_ref, query2_ref, query3_ref,
    keys_ref, keys_t_ref, key_up_ref, value_up_ref, out_ref,
    queries_ref, absorbed_ref, *, softmax_scale, rope_dim, first_head,
):
    tokens = query0_ref.shape[0]
    _, nope_dim, lat_dim = key_up_ref.shape
    value_dim = value_up_ref.shape[2]
    heads = absorbed_ref.shape[0]
    for slot, ref in enumerate((query0_ref, query1_ref, query2_ref, query3_ref)):
        queries_ref[slot * tokens : (slot + 1) * tokens, :] = ref[...]
    absorb_into(queries_ref, key_up_ref, absorbed_ref, first_head, nope_dim, rope_dim)
    for slot in range(4):
        rows = slice(slot * tokens, (slot + 1) * tokens)
        latent_out = attention(
            absorbed_ref[:, rows, :], keys_ref, keys_t_ref,
            hide_of(start_ref, prefix_ref, slot, 0, tokens, tokens, keys_ref.shape[0]),
            softmax_scale, lat_dim,
        )
        for head in range(heads):
            out_ref[rows, head * value_dim : (head + 1) * value_dim] = jnp.dot(
                latent_out[head], value_up_ref[first_head + head],
                preferred_element_type=jnp.float32,
            ).astype(out_ref.dtype)


def attend_everywhere(spans, query_slots, keys, key_up, value_up, softmax_scale, rope_dim):
    tokens, width = query_slots[0].shape
    heads = width // (key_up.shape[1] + rope_dim)
    _, lat_dim, value_dim = value_up.shape
    context, key_width = keys[0].shape
    return pl.pallas_call(
        functools.partial(
            everywhere_kernel,
            softmax_scale=softmax_scale,
            rope_dim=rope_dim,
            first_head=key_up.shape[0] - heads,
        ),
        in_specs=[SMEM] * 2 + [VMEM] * 8,
        out_specs=VMEM,
        scratch_shapes=[
            pltpu.VMEM((4 * tokens, width), key_up.dtype),
            pltpu.VMEM((heads, 4 * tokens, key_width), key_up.dtype),
        ],
        out_shape=jax.ShapeDtypeStruct((4 * tokens, heads * value_dim), key_up.dtype),
        compiler_params=pltpu.CompilerParams(vmem_limit_bytes=24 << 20),
        cost_estimate=pl.CostEstimate(
            flops=8 * tokens * heads * (context * (key_width + lat_dim) + 2 * lat_dim * value_dim),
            bytes_accessed=8 * tokens * (width + heads * value_dim),
            transcendentals=4 * heads * tokens * context,
        ),
    )(*spans, *query_slots, *keys, key_up, value_up)


def project_kernel(
    own_ref, near_ref, far_ref, cross_ref, everywhere_ref, weight_ref, keep_ref, send_ref,
    rows_ref, sums_ref, *, first_token, first_column,
):
    tokens, split = own_ref.shape
    block = everywhere_ref.shape[0] // 4
    columns = keep_ref.shape[1]
    column_block = sums_ref.shape[2]
    for slot, ref in enumerate((own_ref, near_ref, far_ref, cross_ref)):
        rows = slice(slot * tokens, (slot + 1) * tokens)
        first = slot * block + first_token
        rows_ref[rows, :split] = ref[...]
        rows_ref[rows, split:] = everywhere_ref[first : first + tokens, :]
    here = lax.axis_index("seq")
    parity = here % 2
    kept = jnp.where(here // 2 == lax.axis_index("head"), 0, 2)
    for base in range(0, columns, column_block):
        product = jnp.dot(
            rows_ref[...],
            weight_ref[:, first_column + base : first_column + base + column_block],
            preferred_element_type=jnp.float32,
        )
        sums_ref[...] = product.reshape(sums_ref.shape)
        for part in range(2):
            offset = parity if part == 0 else 1 - parity
            rows = slice(part * tokens, (part + 1) * tokens)
            target = slice(base, base + column_block)
            keep_ref[rows, target] = sums_ref[kept + offset]
            send_ref[rows, target] = sums_ref[2 - kept + offset].astype(send_ref.dtype)


def project(slots, everywhere, weight, first_token, first_column, columns, column_block):
    tokens = slots[0].shape[0]
    depth = weight.shape[0]
    return pl.pallas_call(
        functools.partial(project_kernel, first_token=first_token, first_column=first_column),
        in_specs=[VMEM] * 6,
        out_specs=[VMEM] * 2,
        scratch_shapes=[
            pltpu.VMEM((4 * tokens, depth), weight.dtype),
            pltpu.VMEM((4, tokens, column_block), jnp.float32),
        ],
        out_shape=[
            jax.ShapeDtypeStruct((2 * tokens, columns), jnp.float32),
            jax.ShapeDtypeStruct((2 * tokens, columns), weight.dtype),
        ],
        compiler_params=pltpu.CompilerParams(vmem_limit_bytes=12 << 20),
        cost_estimate=pl.CostEstimate(
            flops=8 * tokens * depth * columns,
            bytes_accessed=2 * (depth * columns + 4 * tokens * depth + 6 * tokens * columns),
            transcendentals=0,
        ),
    )(*slots, everywhere, weight)


def finish_kernel(*refs, firsts, aliased):
    count = len(firsts)
    out_ref, sums_ref, sems = refs[-3:]
    refs = refs[aliased : aliased + 2 * count]
    half = out_ref.shape[0] // 2
    copies = []
    done = 0
    for index, first in enumerate(firsts):
        keep_ref, came_ref = refs[index], refs[count + index]
        tokens = keep_ref.shape[0] // 2
        sums_ref[done : done + 2 * tokens, :] = (
            keep_ref[...] + came_ref[...].astype(jnp.float32)
        ).astype(sums_ref.dtype)
        for part in range(2):
            copies.append(
                pltpu.make_async_copy(
                    sums_ref.at[pl.ds(done + part * tokens, tokens), :],
                    out_ref.at[pl.ds(part * half + first, tokens), :],
                    sems.at[2 * index + part],
                )
            )
            copies[-1].start()
        done += 2 * tokens
    for copy in copies:
        copy.wait()


def finish(partial, kept, came, firsts, rows):
    columns = kept[0].shape[1]
    before = [] if partial is None else [partial]
    return pl.pallas_call(
        functools.partial(finish_kernel, firsts=firsts, aliased=len(before)),
        in_specs=[pl.BlockSpec(memory_space=pl.ANY)] * len(before) + [VMEM] * (2 * len(kept)),
        out_specs=pl.BlockSpec(memory_space=pl.ANY),
        scratch_shapes=[
            pltpu.VMEM((sum(keep.shape[0] for keep in kept), columns), came[0].dtype),
            pltpu.SemaphoreType.DMA((2 * len(kept),)),
        ],
        out_shape=jax.ShapeDtypeStruct((rows, columns), came[0].dtype),
        input_output_aliases={0: 0} if before else {},
        compiler_params=pltpu.CompilerParams(vmem_limit_bytes=4 << 20),
        cost_estimate=pl.CostEstimate(
            flops=sum(keep.size for keep in kept),
            bytes_accessed=8 * sum(keep.size for keep in kept),
            transcendentals=0,
        ),
    )(*before, *kept, *came)


def on_device_pairs(
    q_heads, cache_latent, cache_rope, span_start, prefix_len, key_up, value_up, out_weight
):
    queries = q_heads[0]
    tokens = queries.shape[0]
    head_count, nope_dim = key_up.shape[1:3]
    rope_dim = cache_rope.shape[2]
    head_width = nope_dim + rope_dim
    softmax_scale = head_width ** (-0.5)
    columns = out_weight.shape[2]
    everywhere_heads = head_count // EVERYWHERE_SHARE
    sent_heads = head_count - everywhere_heads
    context = tokens * lax.axis_size("seq")
    spans = (span_start[0], prefix_len[0])
    sizes = [tokens * share // sum(SHARES) for share in SHARES]
    firsts = [sum(sizes[:index]) for index in range(CHUNKS)]
    own, half = prepare(cache_latent[0], cache_rope[0].T)
    far = exchange(half, "seq", 2)
    near = exchange(half, "seq", 1)
    absorbed = absorb(queries, key_up[0], rope_dim, sent_heads)
    cross = exchange(far, "seq", 1)
    near_x = exchange(near, "head", 1)
    far_x = exchange(far, "head", 1)
    cross_x = exchange(cross, "head", 1)
    keys = [own, near, far, cross, near_x, far_x, cross_x]
    own = queries[:, sent_heads * head_width :]
    far = exchange(own, "seq", 2)
    near = exchange(own, "seq", 1)
    cross = exchange(far, "seq", 1)
    query_slots = [own, near, far, cross]
    parts = []
    for index in range(CHUNKS):
        own, *rest = attend(
            spans, absorbed, keys, value_up[0], softmax_scale, firsts[index],
            sizes[index], context,
        )
        keys = rest or keys
        far = exchange(own, "seq", 2)
        near = exchange(own, "seq", 1)
        if DIRECT[index]:
            cross = exchange(own, "seq", 3)
        else:
            cross = exchange(far, "seq", 1)
        parts.append([own, near, far, cross])
    everywhere = attend_everywhere(
        spans, query_slots, keys, key_up[0], value_up[0], softmax_scale, rope_dim
    )
    kept, came = [], []
    for index, slots in enumerate(parts):
        keep, sent = project(
            slots, everywhere, out_weight[0], firsts[index], 0, columns, columns // 2
        )
        kept.append(keep)
        came.append(exchange(sent, "head", 1))
    out = finish(None, kept[:-1], came[:-1], firsts[:-1], 2 * tokens)
    out = finish(out, kept[-1:], came[-1:], firsts[-1:], 2 * tokens)
    return out[None]


def on_device_any(
    q_heads, cache_latent, cache_rope, span_start, prefix_len, key_up, value_up, out_weight
):
    queries_flat = q_heads[0]
    tokens = queries_flat.shape[0]
    head_count = key_up.shape[1]
    nope_dim = key_up.shape[2]
    head_width = queries_flat.shape[1] // head_count
    seq_count = lax.axis_size("seq")
    seq_index = lax.axis_index("seq")
    queries = queries_flat.reshape(tokens, head_count, head_width)
    absorbed = jnp.einsum(
        "thn,hnl->thl", queries[:, :, :nope_dim], key_up[0], preferred_element_type=jnp.float32
    ).astype(jnp.bfloat16)
    rope_query = queries[:, :, nope_dim:]
    softmax_scale = head_width ** (-0.5)
    span_len = tokens * seq_count // NSPAN
    global_row = seq_index * tokens + jnp.arange(tokens, dtype=jnp.int32)
    one_hot = (global_row // span_len)[:, None] == jnp.arange(NSPAN, dtype=jnp.int32)[None, :]
    span_first = jnp.sum(jnp.where(one_hot, span_start[0][None, :], 0), axis=1)
    prefix_row = jnp.sum(jnp.where(one_hot, prefix_len[0][None, :], 0), axis=1)
    token_pos = span_first + global_row % span_len
    latent = lax.all_gather(cache_latent[0], "seq", axis=0, tiled=True)
    rope = lax.all_gather(cache_rope[0], "seq", axis=0, tiled=True)
    key_pos = jnp.arange(latent.shape[0], dtype=jnp.int32)
    visible = (
        (key_pos[None, :] < prefix_row[:, None])
        | (key_pos[None, :] >= span_first[:, None]) & (key_pos[None, :] <= token_pos[:, None])
    )[:, None, :]
    scores = jnp.einsum(
        "thl,kl->thk", absorbed, latent, preferred_element_type=jnp.float32
    ) + jnp.einsum("thr,kr->thk", rope_query, rope, preferred_element_type=jnp.float32)
    scores = jnp.where(visible, scores * softmax_scale, masked_fill)
    peak = jnp.max(scores, axis=2, keepdims=True)
    weights = jnp.where(visible, jnp.exp(scores - peak), 0.0)
    totals = jnp.sum(weights, axis=2)
    summed = jnp.einsum(
        "thk,kl->thl", weights.astype(jnp.bfloat16), latent, preferred_element_type=jnp.float32
    )
    latent_out = (summed / totals[:, :, None]).astype(jnp.bfloat16)
    head_out = (
        jnp.einsum("thl,hlv->thv", latent_out, value_up[0], preferred_element_type=jnp.float32)
        .astype(jnp.bfloat16)
        .reshape(tokens, -1)
    )
    partial_out = jnp.dot(
        lax.all_gather(head_out, "seq", axis=0, tiled=True),
        out_weight[0],
        preferred_element_type=jnp.float32,
    )
    mixed_out = lax.psum_scatter(partial_out, "head", scatter_dimension=0, tiled=True)
    return mixed_out.astype(jnp.bfloat16)[None]


def solution(mesh):
    in_specs = (
        P("section", ("groups", "seq"), "head"),
        P("section", ("groups", "seq"), None),
        P("section", ("groups", "seq"), None),
        P("section", "groups"),
        P("section", "groups"),
        P("section", "head", None, None),
        P("section", "head", None, None),
        P("section", "head", "seq"),
    )
    out_specs = P("section", ("groups", "head"), "seq")
    paired = mesh.shape["seq"] == 4 and mesh.shape["head"] == 2
    return jax.shard_map(
        on_device_pairs if paired else on_device_any,
        mesh=mesh, in_specs=in_specs, out_specs=out_specs, check_vma=False,
    )
```

profile of v0, /device:TPU:0, one launch (start us, length us, event | category | flops | bytes accessed | tf_op | source)
XLA Modules:
  0.0 105.3 jit_solution(14920752333509689873)
XLA Ops:
  1.8 4.1 %collective-permute-start.1 = (bf16[64,640]{1,0:T(8,128)(2,1)S(1)}, bf16[64,640]{1,0:T(8,128)(2,1)S(1)}, u32[]{:S(2)}, u32[]{:S(2)}) collective-permute-start(bf16[64,640]{1,0:T(8,128)(2,1)S(1)} %get-tuple-element.19), channel_id=1, source_target_pairs={{0,8},{4,12},{8,0},{12,4},{1,9},{5,13},{9,1},{13,5},{2,10},{6,14},... | collective-permute-start | bytes 245768 | tf_op jit(solution)/shard_map/ppermute | solution.py:27
  7.5 2.2 %collective-permute-done.1.refs_2_ = bf16[64,640]{1,0:T(8,128)(2,1)S(1)} collective-permute-done((bf16[64,640]{1,0:T(8,128)(2,1)S(1)}, bf16[64,640]{1,0:T(8,128)(2,1)S(1)}, u32[]{:S(2)}, u32[]{:S(2)}) %collective-permute-start.1) | collective-permute-done | bytes 81952 | tf_op jit(solution)/shard_map/ppermute | solution.py:27
  14.1 1.9 %collective-permute-start.5 = (bf16[64,640]{1,0:T(8,128)(2,1)S(1)}, bf16[64,640]{1,0:T(8,128)(2,1)S(1)}, u32[]{:S(2)}, u32[]{:S(2)}) collective-permute-start(bf16[64,640]{1,0:T(8,128)(2,1)S(1)} %collective-permute-done.2.refs_3_), channel_id=1, source_target_pairs={{0,2},{2,0},{1,3},{3,1},{4,6},{6,4},{5,7},{7,5},{8,10},{10,8},{9,1... | collective-permute-start | bytes 245768 | tf_op jit(solution)/shard_map/ppermute | solution.py:27
  16.0 2.3 %collective-permute-start.10 = (bf16[128,768]{1,0:T(8,128)(2,1)S(1)}, bf16[128,768]{1,0:T(8,128)(2,1)S(1)}, u32[]{:S(2)}, u32[]{:S(2)}) collective-permute-start(bf16[128,768]{1,0:T(8,128)(2,1)S(1)} %slice.4.query0_ref), channel_id=1, source_target_pairs={{0,8},{4,12},{8,0},{12,4},{1,9},{5,13},{9,1},{13,5},{2,10},{6,14},... | collective-permute-start | bytes 589832 | tf_op jit(solution)/shard_map/ppermute | solution.py:27
  20.4 2.9 %shard_map.84 = (bf16[32,3584]{1,0:T(8,128)(2,1)S(1)}, bf16[512,640]{1,0:T(8,128)(2,1)S(1)}, bf16[640,512]{1,0:T(8,128)(2,1)S(1)}) custom-call(s32[2]{0:T(128)S(1)} %bitcast.26, s32[2]{0:T(128)S(1)} %bitcast.31, bf16[28,128,640]{2,1,0:T(8,128)(2,1)S(1)} %shard_map.82.query_ref, bf16[32,512,128]{2,1,0:T(8,128)(2,1)S(1)} %bitcast.17, ...), custom_call_target="tpu_custom_call" | custom-call | flops 1174405120 | bytes 5570560 | tf_op jit(solution)/shard_map/pallas_call | solution.py:195
  23.3 2.8 %shard_map.87.own_ref = bf16[32,3584]{1,0:T(8,128)(2,1)S(1)} custom-call(s32[2]{0:T(128)S(1)} %bitcast.27, s32[2]{0:T(128)S(1)} %bitcast.32, bf16[28,128,640]{2,1,0:T(8,128)(2,1)S(1)} %shard_map.82.query_ref, bf16[32,512,128]{2,1,0:T(8,128)(2,1)S(1)} %bitcast.18, bf16[512,640]{1,0:T(8,128)(2,1)S(1)} %get-tuple-element.21.keys_ref.refs_0_, ...), custom_call_target="tpu_custom_call" | custom-call | flops 1174405120 | bytes 5570560 | tf_op jit(solution)/shard_map/pallas_call | solution.py:195
  28.8 2.7 %shard_map.89.own_ref = bf16[32,3584]{1,0:T(8,128)(2,1)S(1)} custom-call(s32[2]{0:T(128)S(1)} %bitcast.28, s32[2]{0:T(128)S(1)} %bitcast.33, bf16[28,128,640]{2,1,0:T(8,128)(2,1)S(1)} %shard_map.82.query_ref, bf16[32,512,128]{2,1,0:T(8,128)(2,1)S(1)} %bitcast.19, bf16[512,640]{1,0:T(8,128)(2,1)S(1)} %get-tuple-element.21.keys_ref.refs_0_, ...), custom_call_target="tpu_custom_call" | custom-call | flops 1174405120 | bytes 5570560 | tf_op jit(solution)/shard_map/pallas_call | solution.py:195
  31.6 2.3 %collective-permute-start.16 = (bf16[32,3584]{1,0:T(8,128)(2,1)S(1)}, bf16[32,3584]{1,0:T(8,128)(2,1)S(1)}, u32[]{:S(2)}, u32[]{:S(2)}) collective-permute-start(bf16[32,3584]{1,0:T(8,128)(2,1)S(1)} %shard_map.89.own_ref), channel_id=1, source_target_pairs={{0,8},{4,12},{8,0},{12,4},{1,9},{5,13},{9,1},{13,5},{2,10},{6,14},... | collective-permute-start | bytes 688136 | tf_op jit(solution)/shard_map/ppermute | solution.py:27
  34.0 2.0 %collective-permute-start.11 = (bf16[128,768]{1,0:T(8,128)(2,1)S(1)}, bf16[128,768]{1,0:T(8,128)(2,1)S(1)}, u32[]{:S(2)}, u32[]{:S(2)}) collective-permute-start(bf16[128,768]{1,0:T(8,128)(2,1)S(1)} %collective-permute-done.10.query2_ref), channel_id=1, source_target_pairs={{0,4},{4,0},{8,12},{12,8},{1,5},{5,1},{9,13},{13,9},{2,6},{6,2},{1... | collective-permute-start | bytes 589832 | tf_op jit(solution)/shard_map/ppermute | solution.py:27
  35.9 2.7 %shard_map.92.own_ref = bf16[32,3584]{1,0:T(8,128)(2,1)S(1)} custom-call(s32[2]{0:T(128)S(1)} %bitcast.29, s32[2]{0:T(128)S(1)} %bitcast.34, bf16[28,128,640]{2,1,0:T(8,128)(2,1)S(1)} %shard_map.82.query_ref, bf16[32,512,128]{2,1,0:T(8,128)(2,1)S(1)} %bitcast.20, bf16[512,640]{1,0:T(8,128)(2,1)S(1)} %get-tuple-element.21.keys_ref.refs_0_, ...), custom_call_target="tpu_custom_call" | custom-call | flops 1174405120 | bytes 5570560 | tf_op jit(solution)/shard_map/pallas_call | solution.py:195
  38.7 10.2 %collective-permute-done.9.query1_ref = bf16[128,768]{1,0:T(8,128)(2,1)S(1)} collective-permute-done((bf16[128,768]{1,0:T(8,128)(2,1)S(1)}, bf16[128,768]{1,0:T(8,128)(2,1)S(1)}, u32[]{:S(2)}, u32[]{:S(2)}) %collective-permute-start.9) | collective-permute-done | bytes 196640 | tf_op jit(solution)/shard_map/ppermute | solution.py:27
  50.3 2.8 %collective-permute-done.11.query3_ref = bf16[128,768]{1,0:T(8,128)(2,1)S(1)} collective-permute-done((bf16[128,768]{1,0:T(8,128)(2,1)S(1)}, bf16[128,768]{1,0:T(8,128)(2,1)S(1)}, u32[]{:S(2)}, u32[]{:S(2)}) %collective-permute-start.11) | collective-permute-done | bytes 196640 | tf_op jit(solution)/shard_map/ppermute | solution.py:27
  53.1 2.6 %collective-permute-start.22 = (bf16[32,3584]{1,0:T(8,128)(2,1)S(1)}, bf16[32,3584]{1,0:T(8,128)(2,1)S(1)}, u32[]{:S(2)}, u32[]{:S(2)}) collective-permute-start(bf16[32,3584]{1,0:T(8,128)(2,1)S(1)} %shard_map.92.own_ref), channel_id=1, source_target_pairs={{0,8},{4,12},{8,0},{12,4},{1,9},{5,13},{9,1},{13,5},{2,10},{6,14},... | collective-permute-start | bytes 688136 | tf_op jit(solution)/shard_map/ppermute | solution.py:27
  58.1 5.4 %shard_map.85.everywhere_ref = bf16[512,512]{1,0:T(8,128)(2,1)S(1)} custom-call(s32[2]{0:T(128)S(1)} %bitcast.30, s32[2]{0:T(128)S(1)} %bitcast.35, bf16[128,768]{1,0:T(8,128)(2,1)S(1)} %slice.4.query0_ref, bf16[128,768]{1,0:T(8,128)(2,1)S(1)} %collective-permute-done.9.query1_ref, bf16[128,768]{1,0:T(8,128)(2,1)S(1)} %collective-permute-done.10.query2_ref, ...), custom_call_target="tpu_custom_call" | custom-call | flops 2952790016 | bytes 1310720 | tf_op jit(solution)/shard_map/pallas_call | solution.py:245
  63.5 9.9 %collective-permute-done.7.far_ref = bf16[32,3584]{1,0:T(8,128)(2,1)S(1)} collective-permute-done((bf16[32,3584]{1,0:T(8,128)(2,1)S(1)}, bf16[32,3584]{1,0:T(8,128)(2,1)S(1)}, u32[]{:S(2)}, u32[]{:S(2)}) %collective-permute-start.7) | collective-permute-done | bytes 229408 | tf_op jit(solution)/shard_map/ppermute | solution.py:27
  73.4 2.0 %collective-permute-start.8 = (bf16[32,3584]{1,0:T(8,128)(2,1)S(1)}, bf16[32,3584]{1,0:T(8,128)(2,1)S(1)}, u32[]{:S(2)}, u32[]{:S(2)}) collective-permute-start(bf16[32,3584]{1,0:T(8,128)(2,1)S(1)} %collective-permute-done.7.far_ref), channel_id=1, source_target_pairs={{0,4},{4,0},{8,12},{12,8},{1,5},{5,1},{9,13},{13,9},{2,6},{6,2},{1... | collective-permute-start | bytes 688136 | tf_op jit(solution)/shard_map/ppermute | solution.py:27
  75.4 2.4 %shard_map.88 = (f32[64,1792]{1,0:T(8,128)S(1)}, bf16[64,1792]{1,0:T(8,128)(2,1)S(1)}) custom-call(bf16[32,3584]{1,0:T(8,128)(2,1)S(1)} %shard_map.87.own_ref, bf16[32,3584]{1,0:T(8,128)(2,1)S(1)} %collective-permute-done.12.near_ref, bf16[32,3584]{1,0:T(8,128)(2,1)S(1)} %collective-permute-done.13.far_ref, ...), custom_call_target="tpu_custom_call" | custom-call | flops 1879048192 | bytes 16416768 | tf_op jit(solution)/shard_map/pallas_call | solution.py:302
  78.0 2.0 %collective-permute-start.23 = (bf16[32,3584]{1,0:T(8,128)(2,1)S(1)}, bf16[32,3584]{1,0:T(8,128)(2,1)S(1)}, u32[]{:S(2)}, u32[]{:S(2)}) collective-permute-start(bf16[32,3584]{1,0:T(8,128)(2,1)S(1)} %collective-permute-done.22.far_ref), channel_id=1, source_target_pairs={{0,4},{4,0},{8,12},{12,8},{1,5},{5,1},{9,13},{13,9},{2,6},{6,2},{1... | collective-permute-start | bytes 688136 | tf_op jit(solution)/shard_map/ppermute | solution.py:27
  80.5 2.4 %shard_map.90 = (f32[64,1792]{1,0:T(8,128)S(1)}, bf16[64,1792]{1,0:T(8,128)(2,1)S(1)}) custom-call(bf16[32,3584]{1,0:T(8,128)(2,1)S(1)} %shard_map.89.own_ref, bf16[32,3584]{1,0:T(8,128)(2,1)S(1)} %collective-permute-done.15.near_ref, bf16[32,3584]{1,0:T(8,128)(2,1)S(1)} %collective-permute-done.16.far_ref, ...), custom_call_target="tpu_custom_call" | custom-call | flops 1879048192 | bytes 16416768 | tf_op jit(solution)/shard_map/pallas_call | solution.py:302
  84.6 3.0 %collective-permute-done.8.cross_ref = bf16[32,3584]{1,0:T(8,128)(2,1)S(1)} collective-permute-done((bf16[32,3584]{1,0:T(8,128)(2,1)S(1)}, bf16[32,3584]{1,0:T(8,128)(2,1)S(1)}, u32[]{:S(2)}, u32[]{:S(2)}) %collective-permute-start.8) | collective-permute-done | bytes 229408 | tf_op jit(solution)/shard_map/ppermute | solution.py:27
  87.5 2.4 %shard_map.86 = (f32[64,1792]{1,0:T(8,128)S(1)}, bf16[64,1792]{1,0:T(8,128)(2,1)S(1)}) custom-call(bf16[32,3584]{1,0:T(8,128)(2,1)S(1)} %get-tuple-element.20.own_ref, bf16[32,3584]{1,0:T(8,128)(2,1)S(1)} %collective-permute-done.6.near_ref, bf16[32,3584]{1,0:T(8,128)(2,1)S(1)} %collective-permute-done.7.far_ref, ...), custom_call_target="tpu_custom_call" | custom-call | flops 1879048192 | bytes 16416768 | tf_op jit(solution)/shard_map/pallas_call | solution.py:302
  92.5 3.3 %collective-permute-done.23.cross_ref = bf16[32,3584]{1,0:T(8,128)(2,1)S(1)} collective-permute-done((bf16[32,3584]{1,0:T(8,128)(2,1)S(1)}, bf16[32,3584]{1,0:T(8,128)(2,1)S(1)}, u32[]{:S(2)}, u32[]{:S(2)}) %collective-permute-start.23) | collective-permute-done | bytes 229408 | tf_op jit(solution)/shard_map/ppermute | solution.py:27
  95.8 2.4 %shard_map.93 = (f32[64,1792]{1,0:T(8,128)S(1)}, bf16[64,1792]{1,0:T(8,128)(2,1)S(1)}) custom-call(bf16[32,3584]{1,0:T(8,128)(2,1)S(1)} %shard_map.92.own_ref, bf16[32,3584]{1,0:T(8,128)(2,1)S(1)} %collective-permute-done.21.near_ref, bf16[32,3584]{1,0:T(8,128)(2,1)S(1)} %collective-permute-done.22.far_ref, ...), custom_call_target="tpu_custom_call" | custom-call | flops 1879048192 | bytes 16416768 | tf_op jit(solution)/shard_map/pallas_call | solution.py:302
  99.9 4.5 %collective-permute-done.24.refs_2_ = bf16[64,1792]{1,0:T(8,128)(2,1)S(1)} collective-permute-done((bf16[64,1792]{1,0:T(8,128)(2,1)S(1)}, bf16[64,1792]{1,0:T(8,128)(2,1)S(1)}, u32[]{:S(2)}, u32[]{:S(2)}) %collective-permute-start.24) | collective-permute-done | bytes 229408 | tf_op jit(solution)/shard_map/ppermute | solution.py:27
  (63 shorter events, 23.4 us)
Async XLA Ops:
  1.8 7.9 %collective-permute-start.1 = (bf16[64,640]{1,0:T(8,128)(2,1)S(1)}, bf16[64,640]{1,0:T(8,128)(2,1)S(1)}, u32[]{:S(2)}, u32[]{:S(2)}) collective-permute-start(bf16[64,640]{1,0:T(8,128)(2,1)S(1)} %get-tuple-element.19), channel_id=1, source_target_pairs={{0,8},{4,12},{8,0},{12,4},{1,9},{5,13},{9,1},{13,5},{2,10},{6,14},... | collective-permute-start | bytes 245768 | tf_op jit(solution)/shard_map/ppermute | solution.py:27
  5.9 6.4 %collective-permute-start = (bf16[64,640]{1,0:T(8,128)(2,1)S(1)}, bf16[64,640]{1,0:T(8,128)(2,1)S(1)}, u32[]{:S(2)}, u32[]{:S(2)}) collective-permute-start(bf16[64,640]{1,0:T(8,128)(2,1)S(1)} %get-tuple-element.19), channel_id=1, source_target_pairs={{0,4},{4,0},{8,12},{12,8},{1,5},{5,1},{9,13},{13,9},{2,6},{6,2},{1... | collective-permute-start | bytes 245768 | tf_op jit(solution)/shard_map/ppermute | solution.py:27
  10.8 8.5 %collective-permute-start.4 = (bf16[64,640]{1,0:T(8,128)(2,1)S(1)}, bf16[64,640]{1,0:T(8,128)(2,1)S(1)}, u32[]{:S(2)}, u32[]{:S(2)}) collective-permute-start(bf16[64,640]{1,0:T(8,128)(2,1)S(1)} %collective-permute-done.1.refs_2_), channel_id=1, source_target_pairs={{0,2},{2,0},{1,3},{3,1},{4,6},{6,4},{5,7},{7,5},{8,10},{10,8},{9,1... | collective-permute-start | bytes 245768 | tf_op jit(solution)/shard_map/ppermute | solution.py:27
  12.3 7.1 %collective-permute-start.3 = (bf16[64,640]{1,0:T(8,128)(2,1)S(1)}, bf16[64,640]{1,0:T(8,128)(2,1)S(1)}, u32[]{:S(2)}, u32[]{:S(2)}) collective-permute-start(bf16[64,640]{1,0:T(8,128)(2,1)S(1)} %collective-permute-done.refs_1_), channel_id=1, source_target_pairs={{0,2},{2,0},{1,3},{3,1},{4,6},{6,4},{5,7},{7,5},{8,10},{10,8},{9,1... | collective-permute-start | bytes 245768 | tf_op jit(solution)/shard_map/ppermute | solution.py:27
  14.1 5.3 %collective-permute-start.5 = (bf16[64,640]{1,0:T(8,128)(2,1)S(1)}, bf16[64,640]{1,0:T(8,128)(2,1)S(1)}, u32[]{:S(2)}, u32[]{:S(2)}) collective-permute-start(bf16[64,640]{1,0:T(8,128)(2,1)S(1)} %collective-permute-done.2.refs_3_), channel_id=1, source_target_pairs={{0,2},{2,0},{1,3},{3,1},{4,6},{6,4},{5,7},{7,5},{8,10},{10,8},{9,1... | collective-permute-start | bytes 245768 | tf_op jit(solution)/shard_map/ppermute | solution.py:27
  16.0 18.0 %collective-permute-start.10 = (bf16[128,768]{1,0:T(8,128)(2,1)S(1)}, bf16[128,768]{1,0:T(8,128)(2,1)S(1)}, u32[]{:S(2)}, u32[]{:S(2)}) collective-permute-start(bf16[128,768]{1,0:T(8,128)(2,1)S(1)} %slice.4.query0_ref), channel_id=1, source_target_pairs={{0,8},{4,12},{8,0},{12,4},{1,9},{5,13},{9,1},{13,5},{2,10},{6,14},... | collective-permute-start | bytes 589832 | tf_op jit(solution)/shard_map/ppermute | solution.py:27
  26.1 29.7 %collective-permute-start.13 = (bf16[32,3584]{1,0:T(8,128)(2,1)S(1)}, bf16[32,3584]{1,0:T(8,128)(2,1)S(1)}, u32[]{:S(2)}, u32[]{:S(2)}) collective-permute-start(bf16[32,3584]{1,0:T(8,128)(2,1)S(1)} %shard_map.87.own_ref), channel_id=1, source_target_pairs={{0,8},{4,12},{8,0},{12,4},{1,9},{5,13},{9,1},{13,5},{2,10},{6,14},... | collective-permute-start | bytes 688136 | tf_op jit(solution)/shard_map/ppermute | solution.py:27
  27.7 28.3 %collective-permute-start.12 = (bf16[32,3584]{1,0:T(8,128)(2,1)S(1)}, bf16[32,3584]{1,0:T(8,128)(2,1)S(1)}, u32[]{:S(2)}, u32[]{:S(2)}) collective-permute-start(bf16[32,3584]{1,0:T(8,128)(2,1)S(1)} %shard_map.87.own_ref), channel_id=1, source_target_pairs={{0,4},{4,0},{8,12},{12,8},{1,5},{5,1},{9,13},{13,9},{2,6},{6,2},{1... | collective-permute-start | bytes 688136 | tf_op jit(solution)/shard_map/ppermute | solution.py:27
  31.6 25.8 %collective-permute-start.16 = (bf16[32,3584]{1,0:T(8,128)(2,1)S(1)}, bf16[32,3584]{1,0:T(8,128)(2,1)S(1)}, u32[]{:S(2)}, u32[]{:S(2)}) collective-permute-start(bf16[32,3584]{1,0:T(8,128)(2,1)S(1)} %shard_map.89.own_ref), channel_id=1, source_target_pairs={{0,8},{4,12},{8,0},{12,4},{1,9},{5,13},{9,1},{13,5},{2,10},{6,14},... | collective-permute-start | bytes 688136 | tf_op jit(solution)/shard_map/ppermute | solution.py:27
  33.9 15.0 %collective-permute-start.9 = (bf16[128,768]{1,0:T(8,128)(2,1)S(1)}, bf16[128,768]{1,0:T(8,128)(2,1)S(1)}, u32[]{:S(2)}, u32[]{:S(2)}) collective-permute-start(bf16[128,768]{1,0:T(8,128)(2,1)S(1)} %slice.4.query0_ref), channel_id=1, source_target_pairs={{0,4},{4,0},{8,12},{12,8},{1,5},{5,1},{9,13},{13,9},{2,6},{6,2},{1... | collective-permute-start | bytes 589832 | tf_op jit(solution)/shard_map/ppermute | solution.py:27
  34.0 19.2 %collective-permute-start.11 = (bf16[128,768]{1,0:T(8,128)(2,1)S(1)}, bf16[128,768]{1,0:T(8,128)(2,1)S(1)}, u32[]{:S(2)}, u32[]{:S(2)}) collective-permute-start(bf16[128,768]{1,0:T(8,128)(2,1)S(1)} %collective-permute-done.10.query2_ref), channel_id=1, source_target_pairs={{0,4},{4,0},{8,12},{12,8},{1,5},{5,1},{9,13},{13,9},{2,6},{6,2},{1... | collective-permute-start | bytes 589832 | tf_op jit(solution)/shard_map/ppermute | solution.py:27
  48.9 29.0 %collective-permute-start.15 = (bf16[32,3584]{1,0:T(8,128)(2,1)S(1)}, bf16[32,3584]{1,0:T(8,128)(2,1)S(1)}, u32[]{:S(2)}, u32[]{:S(2)}) collective-permute-start(bf16[32,3584]{1,0:T(8,128)(2,1)S(1)} %shard_map.89.own_ref), channel_id=1, source_target_pairs={{0,4},{4,0},{8,12},{12,8},{1,5},{5,1},{9,13},{13,9},{2,6},{6,2},{1... | collective-permute-start | bytes 688136 | tf_op jit(solution)/shard_map/ppermute | solution.py:27
  53.1 24.9 %collective-permute-start.22 = (bf16[32,3584]{1,0:T(8,128)(2,1)S(1)}, bf16[32,3584]{1,0:T(8,128)(2,1)S(1)}, u32[]{:S(2)}, u32[]{:S(2)}) collective-permute-start(bf16[32,3584]{1,0:T(8,128)(2,1)S(1)} %shard_map.92.own_ref), channel_id=1, source_target_pairs={{0,8},{4,12},{8,0},{12,4},{1,9},{5,13},{9,1},{13,5},{2,10},{6,14},... | collective-permute-start | bytes 688136 | tf_op jit(solution)/shard_map/ppermute | solution.py:27
  55.8 17.6 %collective-permute-start.7 = (bf16[32,3584]{1,0:T(8,128)(2,1)S(1)}, bf16[32,3584]{1,0:T(8,128)(2,1)S(1)}, u32[]{:S(2)}, u32[]{:S(2)}) collective-permute-start(bf16[32,3584]{1,0:T(8,128)(2,1)S(1)} %get-tuple-element.20.own_ref), channel_id=1, source_target_pairs={{0,8},{4,12},{8,0},{12,4},{1,9},{5,13},{9,1},{13,5},{2,10},{6,14},... | collective-permute-start | bytes 688136 | tf_op jit(solution)/shard_map/ppermute | solution.py:27
  56.1 17.3 %collective-permute-start.14 = (bf16[32,3584]{1,0:T(8,128)(2,1)S(1)}, bf16[32,3584]{1,0:T(8,128)(2,1)S(1)}, u32[]{:S(2)}, u32[]{:S(2)}) collective-permute-start(bf16[32,3584]{1,0:T(8,128)(2,1)S(1)} %collective-permute-done.13.far_ref), channel_id=1, source_target_pairs={{0,4},{4,0},{8,12},{12,8},{1,5},{5,1},{9,13},{13,9},{2,6},{6,2},{1... | collective-permute-start | bytes 688136 | tf_op jit(solution)/shard_map/ppermute | solution.py:27
  57.4 22.6 %collective-permute-start.17 = (bf16[32,3584]{1,0:T(8,128)(2,1)S(1)}, bf16[32,3584]{1,0:T(8,128)(2,1)S(1)}, u32[]{:S(2)}, u32[]{:S(2)}) collective-permute-start(bf16[32,3584]{1,0:T(8,128)(2,1)S(1)} %collective-permute-done.16.far_ref), channel_id=1, source_target_pairs={{0,4},{4,0},{8,12},{12,8},{1,5},{5,1},{9,13},{13,9},{2,6},{6,2},{1... | collective-permute-start | bytes 688136 | tf_op jit(solution)/shard_map/ppermute | solution.py:27
  73.4 9.6 %collective-permute-start.6 = (bf16[32,3584]{1,0:T(8,128)(2,1)S(1)}, bf16[32,3584]{1,0:T(8,128)(2,1)S(1)}, u32[]{:S(2)}, u32[]{:S(2)}) collective-permute-start(bf16[32,3584]{1,0:T(8,128)(2,1)S(1)} %get-tuple-element.20.own_ref), channel_id=1, source_target_pairs={{0,4},{4,0},{8,12},{12,8},{1,5},{5,1},{9,13},{13,9},{2,6},{6,2},{1... | collective-permute-start | bytes 688136 | tf_op jit(solution)/shard_map/ppermute | solution.py:27
  73.4 14.1 %collective-permute-start.8 = (bf16[32,3584]{1,0:T(8,128)(2,1)S(1)}, bf16[32,3584]{1,0:T(8,128)(2,1)S(1)}, u32[]{:S(2)}, u32[]{:S(2)}) collective-permute-start(bf16[32,3584]{1,0:T(8,128)(2,1)S(1)} %collective-permute-done.7.far_ref), channel_id=1, source_target_pairs={{0,4},{4,0},{8,12},{12,8},{1,5},{5,1},{9,13},{13,9},{2,6},{6,2},{1... | collective-permute-start | bytes 688136 | tf_op jit(solution)/shard_map/ppermute | solution.py:27
  77.9 14.5 %collective-permute-start.21 = (bf16[32,3584]{1,0:T(8,128)(2,1)S(1)}, bf16[32,3584]{1,0:T(8,128)(2,1)S(1)}, u32[]{:S(2)}, u32[]{:S(2)}) collective-permute-start(bf16[32,3584]{1,0:T(8,128)(2,1)S(1)} %shard_map.92.own_ref), channel_id=1, source_target_pairs={{0,4},{4,0},{8,12},{12,8},{1,5},{5,1},{9,13},{13,9},{2,6},{6,2},{1... | collective-permute-start | bytes 688136 | tf_op jit(solution)/shard_map/ppermute | solution.py:27
  78.0 17.8 %collective-permute-start.23 = (bf16[32,3584]{1,0:T(8,128)(2,1)S(1)}, bf16[32,3584]{1,0:T(8,128)(2,1)S(1)}, u32[]{:S(2)}, u32[]{:S(2)}) collective-permute-start(bf16[32,3584]{1,0:T(8,128)(2,1)S(1)} %collective-permute-done.22.far_ref), channel_id=1, source_target_pairs={{0,4},{4,0},{8,12},{12,8},{1,5},{5,1},{9,13},{13,9},{2,6},{6,2},{1... | collective-permute-start | bytes 688136 | tf_op jit(solution)/shard_map/ppermute | solution.py:27
  80.0 18.9 %collective-permute-start.19 = (bf16[64,1792]{1,0:T(8,128)(2,1)S(1)}, bf16[64,1792]{1,0:T(8,128)(2,1)S(1)}, u32[]{:S(2)}, u32[]{:S(2)}) collective-permute-start(bf16[64,1792]{1,0:T(8,128)(2,1)S(1)} %get-tuple-element.27), channel_id=1, source_target_pairs={{0,2},{2,0},{1,3},{3,1},{4,6},{6,4},{5,7},{7,5},{8,10},{10,8},{9,1... | collective-permute-start | bytes 688136 | tf_op jit(solution)/shard_map/ppermute | solution.py:27
  83.0 15.9 %collective-permute-start.20 = (bf16[64,1792]{1,0:T(8,128)(2,1)S(1)}, bf16[64,1792]{1,0:T(8,128)(2,1)S(1)}, u32[]{:S(2)}, u32[]{:S(2)}) collective-permute-start(bf16[64,1792]{1,0:T(8,128)(2,1)S(1)} %get-tuple-element.28), channel_id=1, source_target_pairs={{0,2},{2,0},{1,3},{3,1},{4,6},{6,4},{5,7},{7,5},{8,10},{10,8},{9,1... | collective-permute-start | bytes 688136 | tf_op jit(solution)/shard_map/ppermute | solution.py:27
  90.0 9.0 %collective-permute-start.18 = (bf16[64,1792]{1,0:T(8,128)(2,1)S(1)}, bf16[64,1792]{1,0:T(8,128)(2,1)S(1)}, u32[]{:S(2)}, u32[]{:S(2)}) collective-permute-start(bf16[64,1792]{1,0:T(8,128)(2,1)S(1)} %get-tuple-element.26), channel_id=1, source_target_pairs={{0,2},{2,0},{1,3},{3,1},{4,6},{6,4},{5,7},{7,5},{8,10},{10,8},{9,1... | collective-permute-start | bytes 688136 | tf_op jit(solution)/shard_map/ppermute | solution.py:27
  98.2 6.1 %collective-permute-start.24 = (bf16[64,1792]{1,0:T(8,128)(2,1)S(1)}, bf16[64,1792]{1,0:T(8,128)(2,1)S(1)}, u32[]{:S(2)}, u32[]{:S(2)}) collective-permute-start(bf16[64,1792]{1,0:T(8,128)(2,1)S(1)} %get-tuple-element.30), channel_id=1, source_target_pairs={{0,2},{2,0},{1,3},{3,1},{4,6},{6,4},{5,7},{7,5},{8,10},{10,8},{9,1... | collective-permute-start | bytes 688136 | tf_op jit(solution)/shard_map/ppermute | solution.py:27
  (12 other events, 200.3 us)
where the time goes:
time: 105 us
  waiting for transfers between devices  38.9 us (37%)
  starting transfers between devices  34.1 us (32%)
  Pallas kernels  29.2 us (28%)
  local copies, waits for them, and re-layouts  2.69 us (3%)
    ppermute x25, waiting for transfers between devices, exchange(): return lax.ppermute(value, axis, [(i, i ^ distance) for i in range(count)])  38.9 us
    ppermute x25, starting transfers between devices, exchange(): return lax.ppermute(value, axis, [(i, i ^ distance) for i in range(count)])  34.1 us
    pallas_call x4, Pallas kernels, attend(): pl.pallas_call(functools.partial(attend_kernel, softmax_scale=softmax_sca...  11.1 us
    pallas_call x4, Pallas kernels, project(): pl.pallas_call(functools.partial(project_kernel, first_token=first_token,...  9.79 us
    pallas_call x1, Pallas kernels, attend_everywhere(): pl.pallas_call(functools.partial(everywhere_kernel, softmax_scale=softmax...  5.36 us
    unnamed x22, local copies, waits for them, and re-layouts  2.67 us
  transfers between devices with their start and end apart: 25, of which 9 were waited for; matrix products, arithmetic and copies ran while one was open for 0% of the time, Pallas kernels for 27%

commit v1 on v0

--- a/solution.py
+++ b/solution.py
@@ -330,10 +330,11 @@
     for index, first in enumerate(firsts):
         keep_ref, came_ref = refs[index], refs[count + index]
         tokens = keep_ref.shape[0] // 2
-        sums_ref[done : done + 2 * tokens, :] = (
-            keep_ref[...] + came_ref[...].astype(jnp.float32)
-        ).astype(sums_ref.dtype)
         for part in range(2):
+            rows = slice(part * tokens, (part + 1) * tokens)
+            sums_ref[done + part * tokens : done + (part + 1) * tokens, :] = (
+                keep_ref[rows, :] + came_ref[rows, :].astype(jnp.float32)
+            ).astype(sums_ref.dtype)
             copies.append(
                 pltpu.make_async_copy(
                     sums_ref.at[pl.ds(done + part * tokens, tokens), :],
@@ -385,7 +386,10 @@
     spans = (span_start[0], prefix_len[0])
     sizes = [tokens * share // sum(SHARES) for share in SHARES]
     firsts = [sum(sizes[:index]) for index in range(CHUNKS)]
-    own, half = prepare(cache_latent[0], cache_rope[0].T)
+    own, half = prepare(
+        pltpu.with_memory_space_constraint(cache_latent[0], pltpu.HBM),
+        pltpu.with_memory_space_constraint(cache_rope[0].T, pltpu.HBM),
+    )
     far = exchange(half, "seq", 2)
     near = exchange(half, "seq", 1)
     absorbed = absorb(queries, key_up[0], rope_dim, sent_heads)

time: 105 us -> 105 us (level)
  local copies, waits for them, and re-layouts: 2.69 us -> 1.07 us
    unnamed x22 -> x18, local copies, waits for them, and re-layouts: 2.67 us -> 1.05 us
where the time goes in v1:
time: 105 us
  waiting for transfers between devices  38.9 us (37%)
  starting transfers between devices  34.1 us (32%)
  Pallas kernels  30.1 us (29%)
  local copies, waits for them, and re-layouts  1.07 us (1%)
    ppermute x25, waiting for transfers between devices, exchange(): return lax.ppermute(value, axis, [(i, i ^ distance) for i in range(count)])  38.9 us
    ppermute x25, starting transfers between devices, exchange(): return lax.ppermute(value, axis, [(i, i ^ distance) for i in range(count)])  34.1 us
    pallas_call x4, Pallas kernels, attend(): pl.pallas_call(functools.partial(attend_kernel, softmax_scale=softmax_sca...  11.1 us
    pallas_call x4, Pallas kernels, project(): pl.pallas_call(functools.partial(project_kernel, first_token=first_token,...  9.79 us
    pallas_call x1, Pallas kernels, attend_everywhere(): pl.pallas_call(functools.partial(everywhere_kernel, softmax_scale=softmax...  5.36 us
  transfers between devices with their start and end apart: 25, of which 9 were waited for; matrix products, arithmetic and copies ran while one was open for 0% of the time, Pallas kernels for 27%

profile of v1, /device:TPU:0, one launch (start us, length us, event | category | flops | bytes accessed | tf_op | source)
XLA Modules:
  0.0 104.6 jit_solution(2910998425127199210)
XLA Ops:
  1.1 4.1 %collective-permute-start.1 = (bf16[64,640]{1,0:T(8,128)(2,1)S(1)}, bf16[64,640]{1,0:T(8,128)(2,1)S(1)}, u32[]{:S(2)}, u32[]{:S(2)}) collective-permute-start(bf16[64,640]{1,0:T(8,128)(2,1)S(1)} %get-tuple-element.19), channel_id=1, source_target_pairs={{0,8},{4,12},{8,0},{12,4},{1,9},{5,13},{9,1},{13,5},{2,10},{6,14},... | collective-permute-start | bytes 245768 | tf_op jit(solution)/shard_map/ppermute | solution.py:27
  6.8 2.2 %collective-permute-done.1.refs_2_ = bf16[64,640]{1,0:T(8,128)(2,1)S(1)} collective-permute-done((bf16[64,640]{1,0:T(8,128)(2,1)S(1)}, bf16[64,640]{1,0:T(8,128)(2,1)S(1)}, u32[]{:S(2)}, u32[]{:S(2)}) %collective-permute-start.1) | collective-permute-done | bytes 81952 | tf_op jit(solution)/shard_map/ppermute | solution.py:27
  13.4 1.9 %collective-permute-start.5 = (bf16[64,640]{1,0:T(8,128)(2,1)S(1)}, bf16[64,640]{1,0:T(8,128)(2,1)S(1)}, u32[]{:S(2)}, u32[]{:S(2)}) collective-permute-start(bf16[64,640]{1,0:T(8,128)(2,1)S(1)} %collective-permute-done.2.refs_3_), channel_id=1, source_target_pairs={{0,2},{2,0},{1,3},{3,1},{4,6},{6,4},{5,7},{7,5},{8,10},{10,8},{9,1... | collective-permute-start | bytes 245768 | tf_op jit(solution)/shard_map/ppermute | solution.py:27
  15.3 2.3 %collective-permute-start.10 = (bf16[128,768]{1,0:T(8,128)(2,1)S(1)}, bf16[128,768]{1,0:T(8,128)(2,1)S(1)}, u32[]{:S(2)}, u32[]{:S(2)}) collective-permute-start(bf16[128,768]{1,0:T(8,128)(2,1)S(1)} %slice.4.query0_ref), channel_id=1, source_target_pairs={{0,8},{4,12},{8,0},{12,4},{1,9},{5,13},{9,1},{13,5},{2,10},{6,14},... | collective-permute-start | bytes 589832 | tf_op jit(solution)/shard_map/ppermute | solution.py:27
  19.8 2.9 %shard_map.84 = (bf16[32,3584]{1,0:T(8,128)(2,1)S(1)}, bf16[512,640]{1,0:T(8,128)(2,1)S(1)}, bf16[640,512]{1,0:T(8,128)(2,1)S(1)}) custom-call(s32[2]{0:T(128)S(1)} %bitcast.26, s32[2]{0:T(128)S(1)} %bitcast.31, bf16[28,128,640]{2,1,0:T(8,128)(2,1)S(1)} %shard_map.82.query_ref, bf16[32,512,128]{2,1,0:T(8,128)(2,1)S(1)} %bitcast.17, ...), custom_call_target="tpu_custom_call" | custom-call | flops 1174405120 | bytes 5570560 | tf_op jit(solution)/shard_map/pallas_call | solution.py:195
  22.7 2.8 %shard_map.87.own_ref = bf16[32,3584]{1,0:T(8,128)(2,1)S(1)} custom-call(s32[2]{0:T(128)S(1)} %bitcast.27, s32[2]{0:T(128)S(1)} %bitcast.32, bf16[28,128,640]{2,1,0:T(8,128)(2,1)S(1)} %shard_map.82.query_ref, bf16[32,512,128]{2,1,0:T(8,128)(2,1)S(1)} %bitcast.18, bf16[512,640]{1,0:T(8,128)(2,1)S(1)} %get-tuple-element.21.keys_ref.refs_0_, ...), custom_call_target="tpu_custom_call" | custom-call | flops 1174405120 | bytes 5570560 | tf_op jit(solution)/shard_map/pallas_call | solution.py:195
  28.2 2.8 %shard_map.89.own_ref = bf16[32,3584]{1,0:T(8,128)(2,1)S(1)} custom-call(s32[2]{0:T(128)S(1)} %bitcast.28, s32[2]{0:T(128)S(1)} %bitcast.33, bf16[28,128,640]{2,1,0:T(8,128)(2,1)S(1)} %shard_map.82.query_ref, bf16[32,512,128]{2,1,0:T(8,128)(2,1)S(1)} %bitcast.19, bf16[512,640]{1,0:T(8,128)(2,1)S(1)} %get-tuple-element.21.keys_ref.refs_0_, ...), custom_call_target="tpu_custom_call" | custom-call | flops 1174405120 | bytes 5570560 | tf_op jit(solution)/shard_map/pallas_call | solution.py:195
  30.9 2.3 %collective-permute-start.16 = (bf16[32,3584]{1,0:T(8,128)(2,1)S(1)}, bf16[32,3584]{1,0:T(8,128)(2,1)S(1)}, u32[]{:S(2)}, u32[]{:S(2)}) collective-permute-start(bf16[32,3584]{1,0:T(8,128)(2,1)S(1)} %shard_map.89.own_ref), channel_id=1, source_target_pairs={{0,8},{4,12},{8,0},{12,4},{1,9},{5,13},{9,1},{13,5},{2,10},{6,14},... | collective-permute-start | bytes 688136 | tf_op jit(solution)/shard_map/ppermute | solution.py:27
  33.3 2.0 %collective-permute-start.11 = (bf16[128,768]{1,0:T(8,128)(2,1)S(1)}, bf16[128,768]{1,0:T(8,128)(2,1)S(1)}, u32[]{:S(2)}, u32[]{:S(2)}) collective-permute-start(bf16[128,768]{1,0:T(8,128)(2,1)S(1)} %collective-permute-done.10.query2_ref), channel_id=1, source_target_pairs={{0,4},{4,0},{8,12},{12,8},{1,5},{5,1},{9,13},{13,9},{2,6},{6,2},{1... | collective-permute-start | bytes 589832 | tf_op jit(solution)/shard_map/ppermute | solution.py:27
  35.3 2.7 %shard_map.92.own_ref = bf16[32,3584]{1,0:T(8,128)(2,1)S(1)} custom-call(s32[2]{0:T(128)S(1)} %bitcast.29, s32[2]{0:T(128)S(1)} %bitcast.34, bf16[28,128,640]{2,1,0:T(8,128)(2,1)S(1)} %shard_map.82.query_ref, bf16[32,512,128]{2,1,0:T(8,128)(2,1)S(1)} %bitcast.20, bf16[512,640]{1,0:T(8,128)(2,1)S(1)} %get-tuple-element.21.keys_ref.refs_0_, ...), custom_call_target="tpu_custom_call" | custom-call | flops 1174405120 | bytes 5570560 | tf_op jit(solution)/shard_map/pallas_call | solution.py:195
  38.0 10.2 %collective-permute-done.9.query1_ref = bf16[128,768]{1,0:T(8,128)(2,1)S(1)} collective-permute-done((bf16[128,768]{1,0:T(8,128)(2,1)S(1)}, bf16[128,768]{1,0:T(8,128)(2,1)S(1)}, u32[]{:S(2)}, u32[]{:S(2)}) %collective-permute-start.9) | collective-permute-done | bytes 196640 | tf_op jit(solution)/shard_map/ppermute | solution.py:27
  49.6 2.8 %collective-permute-done.11.query3_ref = bf16[128,768]{1,0:T(8,128)(2,1)S(1)} collective-permute-done((bf16[128,768]{1,0:T(8,128)(2,1)S(1)}, bf16[128,768]{1,0:T(8,128)(2,1)S(1)}, u32[]{:S(2)}, u32[]{:S(2)}) %collective-permute-start.11) | collective-permute-done | bytes 196640 | tf_op jit(solution)/shard_map/ppermute | solution.py:27
  52.5 2.6 %collective-permute-start.22 = (bf16[32,3584]{1,0:T(8,128)(2,1)S(1)}, bf16[32,3584]{1,0:T(8,128)(2,1)S(1)}, u32[]{:S(2)}, u32[]{:S(2)}) collective-permute-start(bf16[32,3584]{1,0:T(8,128)(2,1)S(1)} %shard_map.92.own_ref), channel_id=1, source_target_pairs={{0,8},{4,12},{8,0},{12,4},{1,9},{5,13},{9,1},{13,5},{2,10},{6,14},... | collective-permute-start | bytes 688136 | tf_op jit(solution)/shard_map/ppermute | solution.py:27
  57.4 5.4 %shard_map.85.everywhere_ref = bf16[512,512]{1,0:T(8,128)(2,1)S(1)} custom-call(s32[2]{0:T(128)S(1)} %bitcast.30, s32[2]{0:T(128)S(1)} %bitcast.35, bf16[128,768]{1,0:T(8,128)(2,1)S(1)} %slice.4.query0_ref, bf16[128,768]{1,0:T(8,128)(2,1)S(1)} %collective-permute-done.9.query1_ref, bf16[128,768]{1,0:T(8,128)(2,1)S(1)} %collective-permute-done.10.query2_ref, ...), custom_call_target="tpu_custom_call" | custom-call | flops 2952790016 | bytes 1310720 | tf_op jit(solution)/shard_map/pallas_call | solution.py:245
  62.8 9.9 %collective-permute-done.7.far_ref = bf16[32,3584]{1,0:T(8,128)(2,1)S(1)} collective-permute-done((bf16[32,3584]{1,0:T(8,128)(2,1)S(1)}, bf16[32,3584]{1,0:T(8,128)(2,1)S(1)}, u32[]{:S(2)}, u32[]{:S(2)}) %collective-permute-start.7) | collective-permute-done | bytes 229408 | tf_op jit(solution)/shard_map/ppermute | solution.py:27
  72.7 2.0 %collective-permute-start.8 = (bf16[32,3584]{1,0:T(8,128)(2,1)S(1)}, bf16[32,3584]{1,0:T(8,128)(2,1)S(1)}, u32[]{:S(2)}, u32[]{:S(2)}) collective-permute-start(bf16[32,3584]{1,0:T(8,128)(2,1)S(1)} %collective-permute-done.7.far_ref), channel_id=1, source_target_pairs={{0,4},{4,0},{8,12},{12,8},{1,5},{5,1},{9,13},{13,9},{2,6},{6,2},{1... | collective-permute-start | bytes 688136 | tf_op jit(solution)/shard_map/ppermute | solution.py:27
  74.8 2.4 %shard_map.88 = (f32[64,1792]{1,0:T(8,128)S(1)}, bf16[64,1792]{1,0:T(8,128)(2,1)S(1)}) custom-call(bf16[32,3584]{1,0:T(8,128)(2,1)S(1)} %shard_map.87.own_ref, bf16[32,3584]{1,0:T(8,128)(2,1)S(1)} %collective-permute-done.12.near_ref, bf16[32,3584]{1,0:T(8,128)(2,1)S(1)} %collective-permute-done.13.far_ref, ...), custom_call_target="tpu_custom_call" | custom-call | flops 1879048192 | bytes 16416768 | tf_op jit(solution)/shard_map/pallas_call | solution.py:302
  77.3 2.0 %collective-permute-start.23 = (bf16[32,3584]{1,0:T(8,128)(2,1)S(1)}, bf16[32,3584]{1,0:T(8,128)(2,1)S(1)}, u32[]{:S(2)}, u32[]{:S(2)}) collective-permute-start(bf16[32,3584]{1,0:T(8,128)(2,1)S(1)} %collective-permute-done.22.far_ref), channel_id=1, source_target_pairs={{0,4},{4,0},{8,12},{12,8},{1,5},{5,1},{9,13},{13,9},{2,6},{6,2},{1... | collective-permute-start | bytes 688136 | tf_op jit(solution)/shard_map/ppermute | solution.py:27
  79.9 2.4 %shard_map.90 = (f32[64,1792]{1,0:T(8,128)S(1)}, bf16[64,1792]{1,0:T(8,128)(2,1)S(1)}) custom-call(bf16[32,3584]{1,0:T(8,128)(2,1)S(1)} %shard_map.89.own_ref, bf16[32,3584]{1,0:T(8,128)(2,1)S(1)} %collective-permute-done.15.near_ref, bf16[32,3584]{1,0:T(8,128)(2,1)S(1)} %collective-permute-done.16.far_ref, ...), custom_call_target="tpu_custom_call" | custom-call | flops 1879048192 | bytes 16416768 | tf_op jit(solution)/shard_map/pallas_call | solution.py:302
  83.9 3.0 %collective-permute-done.8.cross_ref = bf16[32,3584]{1,0:T(8,128)(2,1)S(1)} collective-permute-done((bf16[32,3584]{1,0:T(8,128)(2,1)S(1)}, bf16[32,3584]{1,0:T(8,128)(2,1)S(1)}, u32[]{:S(2)}, u32[]{:S(2)}) %collective-permute-start.8) | collective-permute-done | bytes 229408 | tf_op jit(solution)/shard_map/ppermute | solution.py:27
  86.9 2.4 %shard_map.86 = (f32[64,1792]{1,0:T(8,128)S(1)}, bf16[64,1792]{1,0:T(8,128)(2,1)S(1)}) custom-call(bf16[32,3584]{1,0:T(8,128)(2,1)S(1)} %get-tuple-element.20.own_ref, bf16[32,3584]{1,0:T(8,128)(2,1)S(1)} %collective-permute-done.6.near_ref, bf16[32,3584]{1,0:T(8,128)(2,1)S(1)} %collective-permute-done.7.far_ref, ...), custom_call_target="tpu_custom_call" | custom-call | flops 1879048192 | bytes 16416768 | tf_op jit(solution)/shard_map/pallas_call | solution.py:302
  91.8 3.3 %collective-permute-done.23.cross_ref = bf16[32,3584]{1,0:T(8,128)(2,1)S(1)} collective-permute-done((bf16[32,3584]{1,0:T(8,128)(2,1)S(1)}, bf16[32,3584]{1,0:T(8,128)(2,1)S(1)}, u32[]{:S(2)}, u32[]{:S(2)}) %collective-permute-start.23) | collective-permute-done | bytes 229408 | tf_op jit(solution)/shard_map/ppermute | solution.py:27
  95.1 2.4 %shard_map.93 = (f32[64,1792]{1,0:T(8,128)S(1)}, bf16[64,1792]{1,0:T(8,128)(2,1)S(1)}) custom-call(bf16[32,3584]{1,0:T(8,128)(2,1)S(1)} %shard_map.92.own_ref, bf16[32,3584]{1,0:T(8,128)(2,1)S(1)} %collective-permute-done.21.near_ref, bf16[32,3584]{1,0:T(8,128)(2,1)S(1)} %collective-permute-done.22.far_ref, ...), custom_call_target="tpu_custom_call" | custom-call | flops 1879048192 | bytes 16416768 | tf_op jit(solution)/shard_map/pallas_call | solution.py:302
  99.2 4.5 %collective-permute-done.24.refs_2_ = bf16[64,1792]{1,0:T(8,128)(2,1)S(1)} collective-permute-done((bf16[64,1792]{1,0:T(8,128)(2,1)S(1)}, bf16[64,1792]{1,0:T(8,128)(2,1)S(1)}, u32[]{:S(2)}, u32[]{:S(2)}) %collective-permute-start.24) | collective-permute-done | bytes 229408 | tf_op jit(solution)/shard_map/ppermute | solution.py:27
  (59 shorter events, 22.7 us)
Async XLA Ops:
  1.1 7.9 %collective-permute-start.1 = (bf16[64,640]{1,0:T(8,128)(2,1)S(1)}, bf16[64,640]{1,0:T(8,128)(2,1)S(1)}, u32[]{:S(2)}, u32[]{:S(2)}) collective-permute-start(bf16[64,640]{1,0:T(8,128)(2,1)S(1)} %get-tuple-element.19), channel_id=1, source_target_pairs={{0,8},{4,12},{8,0},{12,4},{1,9},{5,13},{9,1},{13,5},{2,10},{6,14},... | collective-permute-start | bytes 245768 | tf_op jit(solution)/shard_map/ppermute | solution.py:27
  5.2 6.4 %collective-permute-start = (bf16[64,640]{1,0:T(8,128)(2,1)S(1)}, bf16[64,640]{1,0:T(8,128)(2,1)S(1)}, u32[]{:S(2)}, u32[]{:S(2)}) collective-permute-start(bf16[64,640]{1,0:T(8,128)(2,1)S(1)} %get-tuple-element.19), channel_id=1, source_target_pairs={{0,4},{4,0},{8,12},{12,8},{1,5},{5,1},{9,13},{13,9},{2,6},{6,2},{1... | collective-permute-start | bytes 245768 | tf_op jit(solution)/shard_map/ppermute | solution.py:27
  10.2 8.5 %collective-permute-start.4 = (bf16[64,640]{1,0:T(8,128)(2,1)S(1)}, bf16[64,640]{1,0:T(8,128)(2,1)S(1)}, u32[]{:S(2)}, u32[]{:S(2)}) collective-permute-start(bf16[64,640]{1,0:T(8,128)(2,1)S(1)} %collective-permute-done.1.refs_2_), channel_id=1, source_target_pairs={{0,2},{2,0},{1,3},{3,1},{4,6},{6,4},{5,7},{7,5},{8,10},{10,8},{9,1... | collective-permute-start | bytes 245768 | tf_op jit(solution)/shard_map/ppermute | solution.py:27
  11.7 7.1 %collective-permute-start.3 = (bf16[64,640]{1,0:T(8,128)(2,1)S(1)}, bf16[64,640]{1,0:T(8,128)(2,1)S(1)}, u32[]{:S(2)}, u32[]{:S(2)}) collective-permute-start(bf16[64,640]{1,0:T(8,128)(2,1)S(1)} %collective-permute-done.refs_1_), channel_id=1, source_target_pairs={{0,2},{2,0},{1,3},{3,1},{4,6},{6,4},{5,7},{7,5},{8,10},{10,8},{9,1... | collective-permute-start | bytes 245768 | tf_op jit(solution)/shard_map/ppermute | solution.py:27
  13.4 5.3 %collective-permute-start.5 = (bf16[64,640]{1,0:T(8,128)(2,1)S(1)}, bf16[64,640]{1,0:T(8,128)(2,1)S(1)}, u32[]{:S(2)}, u32[]{:S(2)}) collective-permute-start(bf16[64,640]{1,0:T(8,128)(2,1)S(1)} %collective-permute-done.2.refs_3_), channel_id=1, source_target_pairs={{0,2},{2,0},{1,3},{3,1},{4,6},{6,4},{5,7},{7,5},{8,10},{10,8},{9,1... | collective-permute-start | bytes 245768 | tf_op jit(solution)/shard_map/ppermute | solution.py:27
  15.3 18.0 %collective-permute-start.10 = (bf16[128,768]{1,0:T(8,128)(2,1)S(1)}, bf16[128,768]{1,0:T(8,128)(2,1)S(1)}, u32[]{:S(2)}, u32[]{:S(2)}) collective-permute-start(bf16[128,768]{1,0:T(8,128)(2,1)S(1)} %slice.4.query0_ref), channel_id=1, source_target_pairs={{0,8},{4,12},{8,0},{12,4},{1,9},{5,13},{9,1},{13,5},{2,10},{6,14},... | collective-permute-start | bytes 589832 | tf_op jit(solution)/shard_map/ppermute | solution.py:27
  25.4 29.7 %collective-permute-start.13 = (bf16[32,3584]{1,0:T(8,128)(2,1)S(1)}, bf16[32,3584]{1,0:T(8,128)(2,1)S(1)}, u32[]{:S(2)}, u32[]{:S(2)}) collective-permute-start(bf16[32,3584]{1,0:T(8,128)(2,1)S(1)} %shard_map.87.own_ref), channel_id=1, source_target_pairs={{0,8},{4,12},{8,0},{12,4},{1,9},{5,13},{9,1},{13,5},{2,10},{6,14},... | collective-permute-start | bytes 688136 | tf_op jit(solution)/shard_map/ppermute | solution.py:27
  27.0 28.3 %collective-permute-start.12 = (bf16[32,3584]{1,0:T(8,128)(2,1)S(1)}, bf16[32,3584]{1,0:T(8,128)(2,1)S(1)}, u32[]{:S(2)}, u32[]{:S(2)}) collective-permute-start(bf16[32,3584]{1,0:T(8,128)(2,1)S(1)} %shard_map.87.own_ref), channel_id=1, source_target_pairs={{0,4},{4,0},{8,12},{12,8},{1,5},{5,1},{9,13},{13,9},{2,6},{6,2},{1... | collective-permute-start | bytes 688136 | tf_op jit(solution)/shard_map/ppermute | solution.py:27
  30.9 25.8 %collective-permute-start.16 = (bf16[32,3584]{1,0:T(8,128)(2,1)S(1)}, bf16[32,3584]{1,0:T(8,128)(2,1)S(1)}, u32[]{:S(2)}, u32[]{:S(2)}) collective-permute-start(bf16[32,3584]{1,0:T(8,128)(2,1)S(1)} %shard_map.89.own_ref), channel_id=1, source_target_pairs={{0,8},{4,12},{8,0},{12,4},{1,9},{5,13},{9,1},{13,5},{2,10},{6,14},... | collective-permute-start | bytes 688136 | tf_op jit(solution)/shard_map/ppermute | solution.py:27
  33.2 15.0 %collective-permute-start.9 = (bf16[128,768]{1,0:T(8,128)(2,1)S(1)}, bf16[128,768]{1,0:T(8,128)(2,1)S(1)}, u32[]{:S(2)}, u32[]{:S(2)}) collective-permute-start(bf16[128,768]{1,0:T(8,128)(2,1)S(1)} %slice.4.query0_ref), channel_id=1, source_target_pairs={{0,4},{4,0},{8,12},{12,8},{1,5},{5,1},{9,13},{13,9},{2,6},{6,2},{1... | collective-permute-start | bytes 589832 | tf_op jit(solution)/shard_map/ppermute | solution.py:27
  33.3 19.2 %collective-permute-start.11 = (bf16[128,768]{1,0:T(8,128)(2,1)S(1)}, bf16[128,768]{1,0:T(8,128)(2,1)S(1)}, u32[]{:S(2)}, u32[]{:S(2)}) collective-permute-start(bf16[128,768]{1,0:T(8,128)(2,1)S(1)} %collective-permute-done.10.query2_ref), channel_id=1, source_target_pairs={{0,4},{4,0},{8,12},{12,8},{1,5},{5,1},{9,13},{13,9},{2,6},{6,2},{1... | collective-permute-start | bytes 589832 | tf_op jit(solution)/shard_map/ppermute | solution.py:27
  48.2 29.0 %collective-permute-start.15 = (bf16[32,3584]{1,0:T(8,128)(2,1)S(1)}, bf16[32,3584]{1,0:T(8,128)(2,1)S(1)}, u32[]{:S(2)}, u32[]{:S(2)}) collective-permute-start(bf16[32,3584]{1,0:T(8,128)(2,1)S(1)} %shard_map.89.own_ref), channel_id=1, source_target_pairs={{0,4},{4,0},{8,12},{12,8},{1,5},{5,1},{9,13},{13,9},{2,6},{6,2},{1... | collective-permute-start | bytes 688136 | tf_op jit(solution)/shard_map/ppermute | solution.py:27
  52.5 24.9 %collective-permute-start.22 = (bf16[32,3584]{1,0:T(8,128)(2,1)S(1)}, bf16[32,3584]{1,0:T(8,128)(2,1)S(1)}, u32[]{:S(2)}, u32[]{:S(2)}) collective-permute-start(bf16[32,3584]{1,0:T(8,128)(2,1)S(1)} %shard_map.92.own_ref), channel_id=1, source_target_pairs={{0,8},{4,12},{8,0},{12,4},{1,9},{5,13},{9,1},{13,5},{2,10},{6,14},... | collective-permute-start | bytes 688136 | tf_op jit(solution)/shard_map/ppermute | solution.py:27
  55.1 17.6 %collective-permute-start.7 = (bf16[32,3584]{1,0:T(8,128)(2,1)S(1)}, bf16[32,3584]{1,0:T(8,128)(2,1)S(1)}, u32[]{:S(2)}, u32[]{:S(2)}) collective-permute-start(bf16[32,3584]{1,0:T(8,128)(2,1)S(1)} %get-tuple-element.20.own_ref), channel_id=1, source_target_pairs={{0,8},{4,12},{8,0},{12,4},{1,9},{5,13},{9,1},{13,5},{2,10},{6,14},... | collective-permute-start | bytes 688136 | tf_op jit(solution)/shard_map/ppermute | solution.py:27
  55.4 17.3 %collective-permute-start.14 = (bf16[32,3584]{1,0:T(8,128)(2,1)S(1)}, bf16[32,3584]{1,0:T(8,128)(2,1)S(1)}, u32[]{:S(2)}, u32[]{:S(2)}) collective-permute-start(bf16[32,3584]{1,0:T(8,128)(2,1)S(1)} %collective-permute-done.13.far_ref), channel_id=1, source_target_pairs={{0,4},{4,0},{8,12},{12,8},{1,5},{5,1},{9,13},{13,9},{2,6},{6,2},{1... | collective-permute-start | bytes 688136 | tf_op jit(solution)/shard_map/ppermute | solution.py:27
  56.8 22.6 %collective-permute-start.17 = (bf16[32,3584]{1,0:T(8,128)(2,1)S(1)}, bf16[32,3584]{1,0:T(8,128)(2,1)S(1)}, u32[]{:S(2)}, u32[]{:S(2)}) collective-permute-start(bf16[32,3584]{1,0:T(8,128)(2,1)S(1)} %collective-permute-done.16.far_ref), channel_id=1, source_target_pairs={{0,4},{4,0},{8,12},{12,8},{1,5},{5,1},{9,13},{13,9},{2,6},{6,2},{1... | collective-permute-start | bytes 688136 | tf_op jit(solution)/shard_map/ppermute | solution.py:27
  72.7 9.6 %collective-permute-start.6 = (bf16[32,3584]{1,0:T(8,128)(2,1)S(1)}, bf16[32,3584]{1,0:T(8,128)(2,1)S(1)}, u32[]{:S(2)}, u32[]{:S(2)}) collective-permute-start(bf16[32,3584]{1,0:T(8,128)(2,1)S(1)} %get-tuple-element.20.own_ref), channel_id=1, source_target_pairs={{0,4},{4,0},{8,12},{12,8},{1,5},{5,1},{9,13},{13,9},{2,6},{6,2},{1... | collective-permute-start | bytes 688136 | tf_op jit(solution)/shard_map/ppermute | solution.py:27
  72.7 14.1 %collective-permute-start.8 = (bf16[32,3584]{1,0:T(8,128)(2,1)S(1)}, bf16[32,3584]{1,0:T(8,128)(2,1)S(1)}, u32[]{:S(2)}, u32[]{:S(2)}) collective-permute-start(bf16[32,3584]{1,0:T(8,128)(2,1)S(1)} %collective-permute-done.7.far_ref), channel_id=1, source_target_pairs={{0,4},{4,0},{8,12},{12,8},{1,5},{5,1},{9,13},{13,9},{2,6},{6,2},{1... | collective-permute-start | bytes 688136 | tf_op jit(solution)/shard_map/ppermute | solution.py:27
  77.2 14.5 %collective-permute-start.21 = (bf16[32,3584]{1,0:T(8,128)(2,1)S(1)}, bf16[32,3584]{1,0:T(8,128)(2,1)S(1)}, u32[]{:S(2)}, u32[]{:S(2)}) collective-permute-start(bf16[32,3584]{1,0:T(8,128)(2,1)S(1)} %shard_map.92.own_ref), channel_id=1, source_target_pairs={{0,4},{4,0},{8,12},{12,8},{1,5},{5,1},{9,13},{13,9},{2,6},{6,2},{1... | collective-permute-start | bytes 688136 | tf_op jit(solution)/shard_map/ppermute | solution.py:27
  77.3 17.8 %collective-permute-start.23 = (bf16[32,3584]{1,0:T(8,128)(2,1)S(1)}, bf16[32,3584]{1,0:T(8,128)(2,1)S(1)}, u32[]{:S(2)}, u32[]{:S(2)}) collective-permute-start(bf16[32,3584]{1,0:T(8,128)(2,1)S(1)} %collective-permute-done.22.far_ref), channel_id=1, source_target_pairs={{0,4},{4,0},{8,12},{12,8},{1,5},{5,1},{9,13},{13,9},{2,6},{6,2},{1... | collective-permute-start | bytes 688136 | tf_op jit(solution)/shard_map/ppermute | solution.py:27
  79.3 18.9 %collective-permute-start.19 = (bf16[64,1792]{1,0:T(8,128)(2,1)S(1)}, bf16[64,1792]{1,0:T(8,128)(2,1)S(1)}, u32[]{:S(2)}, u32[]{:S(2)}) collective-permute-start(bf16[64,1792]{1,0:T(8,128)(2,1)S(1)} %get-tuple-element.27), channel_id=1, source_target_pairs={{0,2},{2,0},{1,3},{3,1},{4,6},{6,4},{5,7},{7,5},{8,10},{10,8},{9,1... | collective-permute-start | bytes 688136 | tf_op jit(solution)/shard_map/ppermute | solution.py:27
  82.3 15.9 %collective-permute-start.20 = (bf16[64,1792]{1,0:T(8,128)(2,1)S(1)}, bf16[64,1792]{1,0:T(8,128)(2,1)S(1)}, u32[]{:S(2)}, u32[]{:S(2)}) collective-permute-start(bf16[64,1792]{1,0:T(8,128)(2,1)S(1)} %get-tuple-element.28), channel_id=1, source_target_pairs={{0,2},{2,0},{1,3},{3,1},{4,6},{6,4},{5,7},{7,5},{8,10},{10,8},{9,1... | collective-permute-start | bytes 688136 | tf_op jit(solution)/shard_map/ppermute | solution.py:27
  89.3 9.0 %collective-permute-start.18 = (bf16[64,1792]{1,0:T(8,128)(2,1)S(1)}, bf16[64,1792]{1,0:T(8,128)(2,1)S(1)}, u32[]{:S(2)}, u32[]{:S(2)}) collective-permute-start(bf16[64,1792]{1,0:T(8,128)(2,1)S(1)} %get-tuple-element.26), channel_id=1, source_target_pairs={{0,2},{2,0},{1,3},{3,1},{4,6},{6,4},{5,7},{7,5},{8,10},{10,8},{9,1... | collective-permute-start | bytes 688136 | tf_op jit(solution)/shard_map/ppermute | solution.py:27
  97.6 6.1 %collective-permute-start.24 = (bf16[64,1792]{1,0:T(8,128)(2,1)S(1)}, bf16[64,1792]{1,0:T(8,128)(2,1)S(1)}, u32[]{:S(2)}, u32[]{:S(2)}) collective-permute-start(bf16[64,1792]{1,0:T(8,128)(2,1)S(1)} %get-tuple-element.30), channel_id=1, source_target_pairs={{0,2},{2,0},{1,3},{3,1},{4,6},{6,4},{5,7},{7,5},{8,10},{10,8},{9,1... | collective-permute-start | bytes 688136 | tf_op jit(solution)/shard_map/ppermute | solution.py:27
  (10 other events, 200.5 us)

commit v2 on v0

--- a/solution.py
+++ b/solution.py
@@ -385,7 +385,10 @@
     spans = (span_start[0], prefix_len[0])
     sizes = [tokens * share // sum(SHARES) for share in SHARES]
     firsts = [sum(sizes[:index]) for index in range(CHUNKS)]
-    own, half = prepare(cache_latent[0], cache_rope[0].T)
+    own, half = prepare(
+        pltpu.with_memory_space_constraint(cache_latent[0], pltpu.HBM),
+        pltpu.with_memory_space_constraint(cache_rope[0].T, pltpu.HBM),
+    )
     far = exchange(half, "seq", 2)
     near = exchange(half, "seq", 1)
     absorbed = absorb(queries, key_up[0], rope_dim, sent_heads)

time: 105 us -> 105 us (level)
  local copies, waits for them, and re-layouts: 2.69 us -> 1.07 us
    unnamed x22 -> x18, local copies, waits for them, and re-layouts: 2.67 us -> 1.05 us
where the time goes in v2:
time: 105 us
  waiting for transfers between devices  38.9 us (37%)
  starting transfers between devices  34.1 us (32%)
  Pallas kernels  30.2 us (29%)
  local copies, waits for them, and re-layouts  1.07 us (1%)
    ppermute x25, waiting for transfers between devices, exchange(): return lax.ppermute(value, axis, [(i, i ^ distance) for i in range(count)])  38.9 us
    ppermute x25, starting transfers between devices, exchange(): return lax.ppermute(value, axis, [(i, i ^ distance) for i in range(count)])  34.1 us
    pallas_call x4, Pallas kernels, attend(): pl.pallas_call(functools.partial(attend_kernel, softmax_scale=softmax_sca...  11.1 us
    pallas_call x4, Pallas kernels, project(): pl.pallas_call(functools.partial(project_kernel, first_token=first_token,...  9.79 us
    pallas_call x1, Pallas kernels, attend_everywhere(): pl.pallas_call(functools.partial(everywhere_kernel, softmax_scale=softmax...  5.36 us
  transfers between devices with their start and end apart: 25, of which 9 were waited for; matrix products, arithmetic and copies ran while one was open for 0% of the time, Pallas kernels for 27%

profile of v2, /device:TPU:0, one launch (start us, length us, event | category | flops | bytes accessed | tf_op | source)
XLA Modules:
  0.0 104.6 jit_solution(2750374794079391812)
XLA Ops:
  1.1 4.1 %collective-permute-start.1 = (bf16[64,640]{1,0:T(8,128)(2,1)S(1)}, bf16[64,640]{1,0:T(8,128)(2,1)S(1)}, u32[]{:S(2)}, u32[]{:S(2)}) collective-permute-start(bf16[64,640]{1,0:T(8,128)(2,1)S(1)} %get-tuple-element.19), channel_id=1, source_target_pairs={{0,8},{4,12},{8,0},{12,4},{1,9},{5,13},{9,1},{13,5},{2,10},{6,14},... | collective-permute-start | bytes 245768 | tf_op jit(solution)/shard_map/ppermute | solution.py:27
  6.8 2.2 %collective-permute-done.1.refs_2_ = bf16[64,640]{1,0:T(8,128)(2,1)S(1)} collective-permute-done((bf16[64,640]{1,0:T(8,128)(2,1)S(1)}, bf16[64,640]{1,0:T(8,128)(2,1)S(1)}, u32[]{:S(2)}, u32[]{:S(2)}) %collective-permute-start.1) | collective-permute-done | bytes 81952 | tf_op jit(solution)/shard_map/ppermute | solution.py:27
  13.4 1.9 %collective-permute-start.5 = (bf16[64,640]{1,0:T(8,128)(2,1)S(1)}, bf16[64,640]{1,0:T(8,128)(2,1)S(1)}, u32[]{:S(2)}, u32[]{:S(2)}) collective-permute-start(bf16[64,640]{1,0:T(8,128)(2,1)S(1)} %collective-permute-done.2.refs_3_), channel_id=1, source_target_pairs={{0,2},{2,0},{1,3},{3,1},{4,6},{6,4},{5,7},{7,5},{8,10},{10,8},{9,1... | collective-permute-start | bytes 245768 | tf_op jit(solution)/shard_map/ppermute | solution.py:27
  15.3 2.3 %collective-permute-start.10 = (bf16[128,768]{1,0:T(8,128)(2,1)S(1)}, bf16[128,768]{1,0:T(8,128)(2,1)S(1)}, u32[]{:S(2)}, u32[]{:S(2)}) collective-permute-start(bf16[128,768]{1,0:T(8,128)(2,1)S(1)} %slice.4.query0_ref), channel_id=1, source_target_pairs={{0,8},{4,12},{8,0},{12,4},{1,9},{5,13},{9,1},{13,5},{2,10},{6,14},... | collective-permute-start | bytes 589832 | tf_op jit(solution)/shard_map/ppermute | solution.py:27
  19.8 2.9 %shard_map.84 = (bf16[32,3584]{1,0:T(8,128)(2,1)S(1)}, bf16[512,640]{1,0:T(8,128)(2,1)S(1)}, bf16[640,512]{1,0:T(8,128)(2,1)S(1)}) custom-call(s32[2]{0:T(128)S(1)} %bitcast.26, s32[2]{0:T(128)S(1)} %bitcast.31, bf16[28,128,640]{2,1,0:T(8,128)(2,1)S(1)} %shard_map.82.query_ref, bf16[32,512,128]{2,1,0:T(8,128)(2,1)S(1)} %bitcast.17, ...), custom_call_target="tpu_custom_call" | custom-call | flops 1174405120 | bytes 5570560 | tf_op jit(solution)/shard_map/pallas_call | solution.py:195
  22.7 2.8 %shard_map.87.own_ref = bf16[32,3584]{1,0:T(8,128)(2,1)S(1)} custom-call(s32[2]{0:T(128)S(1)} %bitcast.27, s32[2]{0:T(128)S(1)} %bitcast.32, bf16[28,128,640]{2,1,0:T(8,128)(2,1)S(1)} %shard_map.82.query_ref, bf16[32,512,128]{2,1,0:T(8,128)(2,1)S(1)} %bitcast.18, bf16[512,640]{1,0:T(8,128)(2,1)S(1)} %get-tuple-element.21.keys_ref.refs_0_, ...), custom_call_target="tpu_custom_call" | custom-call | flops 1174405120 | bytes 5570560 | tf_op jit(solution)/shard_map/pallas_call | solution.py:195
  28.2 2.8 %shard_map.89.own_ref = bf16[32,3584]{1,0:T(8,128)(2,1)S(1)} custom-call(s32[2]{0:T(128)S(1)} %bitcast.28, s32[2]{0:T(128)S(1)} %bitcast.33, bf16[28,128,640]{2,1,0:T(8,128)(2,1)S(1)} %shard_map.82.query_ref, bf16[32,512,128]{2,1,0:T(8,128)(2,1)S(1)} %bitcast.19, bf16[512,640]{1,0:T(8,128)(2,1)S(1)} %get-tuple-element.21.keys_ref.refs_0_, ...), custom_call_target="tpu_custom_call" | custom-call | flops 1174405120 | bytes 5570560 | tf_op jit(solution)/shard_map/pallas_call | solution.py:195
  30.9 2.3 %collective-permute-start.16 = (bf16[32,3584]{1,0:T(8,128)(2,1)S(1)}, bf16[32,3584]{1,0:T(8,128)(2,1)S(1)}, u32[]{:S(2)}, u32[]{:S(2)}) collective-permute-start(bf16[32,3584]{1,0:T(8,128)(2,1)S(1)} %shard_map.89.own_ref), channel_id=1, source_target_pairs={{0,8},{4,12},{8,0},{12,4},{1,9},{5,13},{9,1},{13,5},{2,10},{6,14},... | collective-permute-start | bytes 688136 | tf_op jit(solution)/shard_map/ppermute | solution.py:27
  33.3 2.0 %collective-permute-start.11 = (bf16[128,768]{1,0:T(8,128)(2,1)S(1)}, bf16[128,768]{1,0:T(8,128)(2,1)S(1)}, u32[]{:S(2)}, u32[]{:S(2)}) collective-permute-start(bf16[128,768]{1,0:T(8,128)(2,1)S(1)} %collective-permute-done.10.query2_ref), channel_id=1, source_target_pairs={{0,4},{4,0},{8,12},{12,8},{1,5},{5,1},{9,13},{13,9},{2,6},{6,2},{1... | collective-permute-start | bytes 589832 | tf_op jit(solution)/shard_map/ppermute | solution.py:27
  35.3 2.7 %shard_map.92.own_ref = bf16[32,3584]{1,0:T(8,128)(2,1)S(1)} custom-call(s32[2]{0:T(128)S(1)} %bitcast.29, s32[2]{0:T(128)S(1)} %bitcast.34, bf16[28,128,640]{2,1,0:T(8,128)(2,1)S(1)} %shard_map.82.query_ref, bf16[32,512,128]{2,1,0:T(8,128)(2,1)S(1)} %bitcast.20, bf16[512,640]{1,0:T(8,128)(2,1)S(1)} %get-tuple-element.21.keys_ref.refs_0_, ...), custom_call_target="tpu_custom_call" | custom-call | flops 1174405120 | bytes 5570560 | tf_op jit(solution)/shard_map/pallas_call | solution.py:195
  38.0 10.2 %collective-permute-done.9.query1_ref = bf16[128,768]{1,0:T(8,128)(2,1)S(1)} collective-permute-done((bf16[128,768]{1,0:T(8,128)(2,1)S(1)}, bf16[128,768]{1,0:T(8,128)(2,1)S(1)}, u32[]{:S(2)}, u32[]{:S(2)}) %collective-permute-start.9) | collective-permute-done | bytes 196640 | tf_op jit(solution)/shard_map/ppermute | solution.py:27
  49.6 2.8 %collective-permute-done.11.query3_ref = bf16[128,768]{1,0:T(8,128)(2,1)S(1)} collective-permute-done((bf16[128,768]{1,0:T(8,128)(2,1)S(1)}, bf16[128,768]{1,0:T(8,128)(2,1)S(1)}, u32[]{:S(2)}, u32[]{:S(2)}) %collective-permute-start.11) | collective-permute-done | bytes 196640 | tf_op jit(solution)/shard_map/ppermute | solution.py:27
  52.5 2.6 %collective-permute-start.22 = (bf16[32,3584]{1,0:T(8,128)(2,1)S(1)}, bf16[32,3584]{1,0:T(8,128)(2,1)S(1)}, u32[]{:S(2)}, u32[]{:S(2)}) collective-permute-start(bf16[32,3584]{1,0:T(8,128)(2,1)S(1)} %shard_map.92.own_ref), channel_id=1, source_target_pairs={{0,8},{4,12},{8,0},{12,4},{1,9},{5,13},{9,1},{13,5},{2,10},{6,14},... | collective-permute-start | bytes 688136 | tf_op jit(solution)/shard_map/ppermute | solution.py:27
  57.4 5.4 %shard_map.85.everywhere_ref = bf16[512,512]{1,0:T(8,128)(2,1)S(1)} custom-call(s32[2]{0:T(128)S(1)} %bitcast.30, s32[2]{0:T(128)S(1)} %bitcast.35, bf16[128,768]{1,0:T(8,128)(2,1)S(1)} %slice.4.query0_ref, bf16[128,768]{1,0:T(8,128)(2,1)S(1)} %collective-permute-done.9.query1_ref, bf16[128,768]{1,0:T(8,128)(2,1)S(1)} %collective-permute-done.10.query2_ref, ...), custom_call_target="tpu_custom_call" | custom-call | flops 2952790016 | bytes 1310720 | tf_op jit(solution)/shard_map/pallas_call | solution.py:245
  62.8 9.9 %collective-permute-done.7.far_ref = bf16[32,3584]{1,0:T(8,128)(2,1)S(1)} collective-permute-done((bf16[32,3584]{1,0:T(8,128)(2,1)S(1)}, bf16[32,3584]{1,0:T(8,128)(2,1)S(1)}, u32[]{:S(2)}, u32[]{:S(2)}) %collective-permute-start.7) | collective-permute-done | bytes 229408 | tf_op jit(solution)/shard_map/ppermute | solution.py:27
  72.7 2.0 %collective-permute-start.8 = (bf16[32,3584]{1,0:T(8,128)(2,1)S(1)}, bf16[32,3584]{1,0:T(8,128)(2,1)S(1)}, u32[]{:S(2)}, u32[]{:S(2)}) collective-permute-start(bf16[32,3584]{1,0:T(8,128)(2,1)S(1)} %collective-permute-done.7.far_ref), channel_id=1, source_target_pairs={{0,4},{4,0},{8,12},{12,8},{1,5},{5,1},{9,13},{13,9},{2,6},{6,2},{1... | collective-permute-start | bytes 688136 | tf_op jit(solution)/shard_map/ppermute | solution.py:27
  74.8 2.4 %shard_map.88 = (f32[64,1792]{1,0:T(8,128)S(1)}, bf16[64,1792]{1,0:T(8,128)(2,1)S(1)}) custom-call(bf16[32,3584]{1,0:T(8,128)(2,1)S(1)} %shard_map.87.own_ref, bf16[32,3584]{1,0:T(8,128)(2,1)S(1)} %collective-permute-done.12.near_ref, bf16[32,3584]{1,0:T(8,128)(2,1)S(1)} %collective-permute-done.13.far_ref, ...), custom_call_target="tpu_custom_call" | custom-call | flops 1879048192 | bytes 16416768 | tf_op jit(solution)/shard_map/pallas_call | solution.py:302
  77.3 2.0 %collective-permute-start.23 = (bf16[32,3584]{1,0:T(8,128)(2,1)S(1)}, bf16[32,3584]{1,0:T(8,128)(2,1)S(1)}, u32[]{:S(2)}, u32[]{:S(2)}) collective-permute-start(bf16[32,3584]{1,0:T(8,128)(2,1)S(1)} %collective-permute-done.22.far_ref), channel_id=1, source_target_pairs={{0,4},{4,0},{8,12},{12,8},{1,5},{5,1},{9,13},{13,9},{2,6},{6,2},{1... | collective-permute-start | bytes 688136 | tf_op jit(solution)/shard_map/ppermute | solution.py:27
  79.9 2.4 %shard_map.90 = (f32[64,1792]{1,0:T(8,128)S(1)}, bf16[64,1792]{1,0:T(8,128)(2,1)S(1)}) custom-call(bf16[32,3584]{1,0:T(8,128)(2,1)S(1)} %shard_map.89.own_ref, bf16[32,3584]{1,0:T(8,128)(2,1)S(1)} %collective-permute-done.15.near_ref, bf16[32,3584]{1,0:T(8,128)(2,1)S(1)} %collective-permute-done.16.far_ref, ...), custom_call_target="tpu_custom_call" | custom-call | flops 1879048192 | bytes 16416768 | tf_op jit(solution)/shard_map/pallas_call | solution.py:302
  83.9 3.0 %collective-permute-done.8.cross_ref = bf16[32,3584]{1,0:T(8,128)(2,1)S(1)} collective-permute-done((bf16[32,3584]{1,0:T(8,128)(2,1)S(1)}, bf16[32,3584]{1,0:T(8,128)(2,1)S(1)}, u32[]{:S(2)}, u32[]{:S(2)}) %collective-permute-start.8) | collective-permute-done | bytes 229408 | tf_op jit(solution)/shard_map/ppermute | solution.py:27
  86.9 2.4 %shard_map.86 = (f32[64,1792]{1,0:T(8,128)S(1)}, bf16[64,1792]{1,0:T(8,128)(2,1)S(1)}) custom-call(bf16[32,3584]{1,0:T(8,128)(2,1)S(1)} %get-tuple-element.20.own_ref, bf16[32,3584]{1,0:T(8,128)(2,1)S(1)} %collective-permute-done.6.near_ref, bf16[32,3584]{1,0:T(8,128)(2,1)S(1)} %collective-permute-done.7.far_ref, ...), custom_call_target="tpu_custom_call" | custom-call | flops 1879048192 | bytes 16416768 | tf_op jit(solution)/shard_map/pallas_call | solution.py:302
  91.8 3.3 %collective-permute-done.23.cross_ref = bf16[32,3584]{1,0:T(8,128)(2,1)S(1)} collective-permute-done((bf16[32,3584]{1,0:T(8,128)(2,1)S(1)}, bf16[32,3584]{1,0:T(8,128)(2,1)S(1)}, u32[]{:S(2)}, u32[]{:S(2)}) %collective-permute-start.23) | collective-permute-done | bytes 229408 | tf_op jit(solution)/shard_map/ppermute | solution.py:27
  95.1 2.4 %shard_map.93 = (f32[64,1792]{1,0:T(8,128)S(1)}, bf16[64,1792]{1,0:T(8,128)(2,1)S(1)}) custom-call(bf16[32,3584]{1,0:T(8,128)(2,1)S(1)} %shard_map.92.own_ref, bf16[32,3584]{1,0:T(8,128)(2,1)S(1)} %collective-permute-done.21.near_ref, bf16[32,3584]{1,0:T(8,128)(2,1)S(1)} %collective-permute-done.22.far_ref, ...), custom_call_target="tpu_custom_call" | custom-call | flops 1879048192 | bytes 16416768 | tf_op jit(solution)/shard_map/pallas_call | solution.py:302
  99.2 4.5 %collective-permute-done.24.refs_2_ = bf16[64,1792]{1,0:T(8,128)(2,1)S(1)} collective-permute-done((bf16[64,1792]{1,0:T(8,128)(2,1)S(1)}, bf16[64,1792]{1,0:T(8,128)(2,1)S(1)}, u32[]{:S(2)}, u32[]{:S(2)}) %collective-permute-start.24) | collective-permute-done | bytes 229408 | tf_op jit(solution)/shard_map/ppermute | solution.py:27
  (59 shorter events, 22.8 us)
Async XLA Ops:
  1.1 7.9 %collective-permute-start.1 = (bf16[64,640]{1,0:T(8,128)(2,1)S(1)}, bf16[64,640]{1,0:T(8,128)(2,1)S(1)}, u32[]{:S(2)}, u32[]{:S(2)}) collective-permute-start(bf16[64,640]{1,0:T(8,128)(2,1)S(1)} %get-tuple-element.19), channel_id=1, source_target_pairs={{0,8},{4,12},{8,0},{12,4},{1,9},{5,13},{9,1},{13,5},{2,10},{6,14},... | collective-permute-start | bytes 245768 | tf_op jit(solution)/shard_map/ppermute | solution.py:27
  5.2 6.4 %collective-permute-start = (bf16[64,640]{1,0:T(8,128)(2,1)S(1)}, bf16[64,640]{1,0:T(8,128)(2,1)S(1)}, u32[]{:S(2)}, u32[]{:S(2)}) collective-permute-start(bf16[64,640]{1,0:T(8,128)(2,1)S(1)} %get-tuple-element.19), channel_id=1, source_target_pairs={{0,4},{4,0},{8,12},{12,8},{1,5},{5,1},{9,13},{13,9},{2,6},{6,2},{1... | collective-permute-start | bytes 245768 | tf_op jit(solution)/shard_map/ppermute | solution.py:27
  10.2 8.5 %collective-permute-start.4 = (bf16[64,640]{1,0:T(8,128)(2,1)S(1)}, bf16[64,640]{1,0:T(8,128)(2,1)S(1)}, u32[]{:S(2)}, u32[]{:S(2)}) collective-permute-start(bf16[64,640]{1,0:T(8,128)(2,1)S(1)} %collective-permute-done.1.refs_2_), channel_id=1, source_target_pairs={{0,2},{2,0},{1,3},{3,1},{4,6},{6,4},{5,7},{7,5},{8,10},{10,8},{9,1... | collective-permute-start | bytes 245768 | tf_op jit(solution)/shard_map/ppermute | solution.py:27
  11.7 7.1 %collective-permute-start.3 = (bf16[64,640]{1,0:T(8,128)(2,1)S(1)}, bf16[64,640]{1,0:T(8,128)(2,1)S(1)}, u32[]{:S(2)}, u32[]{:S(2)}) collective-permute-start(bf16[64,640]{1,0:T(8,128)(2,1)S(1)} %collective-permute-done.refs_1_), channel_id=1, source_target_pairs={{0,2},{2,0},{1,3},{3,1},{4,6},{6,4},{5,7},{7,5},{8,10},{10,8},{9,1... | collective-permute-start | bytes 245768 | tf_op jit(solution)/shard_map/ppermute | solution.py:27
  13.4 5.3 %collective-permute-start.5 = (bf16[64,640]{1,0:T(8,128)(2,1)S(1)}, bf16[64,640]{1,0:T(8,128)(2,1)S(1)}, u32[]{:S(2)}, u32[]{:S(2)}) collective-permute-start(bf16[64,640]{1,0:T(8,128)(2,1)S(1)} %collective-permute-done.2.refs_3_), channel_id=1, source_target_pairs={{0,2},{2,0},{1,3},{3,1},{4,6},{6,4},{5,7},{7,5},{8,10},{10,8},{9,1... | collective-permute-start | bytes 245768 | tf_op jit(solution)/shard_map/ppermute | solution.py:27
  15.3 18.0 %collective-permute-start.10 = (bf16[128,768]{1,0:T(8,128)(2,1)S(1)}, bf16[128,768]{1,0:T(8,128)(2,1)S(1)}, u32[]{:S(2)}, u32[]{:S(2)}) collective-permute-start(bf16[128,768]{1,0:T(8,128)(2,1)S(1)} %slice.4.query0_ref), channel_id=1, source_target_pairs={{0,8},{4,12},{8,0},{12,4},{1,9},{5,13},{9,1},{13,5},{2,10},{6,14},... | collective-permute-start | bytes 589832 | tf_op jit(solution)/shard_map/ppermute | solution.py:27
  25.4 29.7 %collective-permute-start.13 = (bf16[32,3584]{1,0:T(8,128)(2,1)S(1)}, bf16[32,3584]{1,0:T(8,128)(2,1)S(1)}, u32[]{:S(2)}, u32[]{:S(2)}) collective-permute-start(bf16[32,3584]{1,0:T(8,128)(2,1)S(1)} %shard_map.87.own_ref), channel_id=1, source_target_pairs={{0,8},{4,12},{8,0},{12,4},{1,9},{5,13},{9,1},{13,5},{2,10},{6,14},... | collective-permute-start | bytes 688136 | tf_op jit(solution)/shard_map/ppermute | solution.py:27
  27.0 28.3 %collective-permute-start.12 = (bf16[32,3584]{1,0:T(8,128)(2,1)S(1)}, bf16[32,3584]{1,0:T(8,128)(2,1)S(1)}, u32[]{:S(2)}, u32[]{:S(2)}) collective-permute-start(bf16[32,3584]{1,0:T(8,128)(2,1)S(1)} %shard_map.87.own_ref), channel_id=1, source_target_pairs={{0,4},{4,0},{8,12},{12,8},{1,5},{5,1},{9,13},{13,9},{2,6},{6,2},{1... | collective-permute-start | bytes 688136 | tf_op jit(solution)/shard_map/ppermute | solution.py:27
  30.9 25.8 %collective-permute-start.16 = (bf16[32,3584]{1,0:T(8,128)(2,1)S(1)}, bf16[32,3584]{1,0:T(8,128)(2,1)S(1)}, u32[]{:S(2)}, u32[]{:S(2)}) collective-permute-start(bf16[32,3584]{1,0:T(8,128)(2,1)S(1)} %shard_map.89.own_ref), channel_id=1, source_target_pairs={{0,8},{4,12},{8,0},{12,4},{1,9},{5,13},{9,1},{13,5},{2,10},{6,14},... | collective-permute-start | bytes 688136 | tf_op jit(solution)/shard_map/ppermute | solution.py:27
  33.2 15.0 %collective-permute-start.9 = (bf16[128,768]{1,0:T(8,128)(2,1)S(1)}, bf16[128,768]{1,0:T(8,128)(2,1)S(1)}, u32[]{:S(2)}, u32[]{:S(2)}) collective-permute-start(bf16[128,768]{1,0:T(8,128)(2,1)S(1)} %slice.4.query0_ref), channel_id=1, source_target_pairs={{0,4},{4,0},{8,12},{12,8},{1,5},{5,1},{9,13},{13,9},{2,6},{6,2},{1... | collective-permute-start | bytes 589832 | tf_op jit(solution)/shard_map/ppermute | solution.py:27
  33.3 19.2 %collective-permute-start.11 = (bf16[128,768]{1,0:T(8,128)(2,1)S(1)}, bf16[128,768]{1,0:T(8,128)(2,1)S(1)}, u32[]{:S(2)}, u32[]{:S(2)}) collective-permute-start(bf16[128,768]{1,0:T(8,128)(2,1)S(1)} %collective-permute-done.10.query2_ref), channel_id=1, source_target_pairs={{0,4},{4,0},{8,12},{12,8},{1,5},{5,1},{9,13},{13,9},{2,6},{6,2},{1... | collective-permute-start | bytes 589832 | tf_op jit(solution)/shard_map/ppermute | solution.py:27
  48.2 29.0 %collective-permute-start.15 = (bf16[32,3584]{1,0:T(8,128)(2,1)S(1)}, bf16[32,3584]{1,0:T(8,128)(2,1)S(1)}, u32[]{:S(2)}, u32[]{:S(2)}) collective-permute-start(bf16[32,3584]{1,0:T(8,128)(2,1)S(1)} %shard_map.89.own_ref), channel_id=1, source_target_pairs={{0,4},{4,0},{8,12},{12,8},{1,5},{5,1},{9,13},{13,9},{2,6},{6,2},{1... | collective-permute-start | bytes 688136 | tf_op jit(solution)/shard_map/ppermute | solution.py:27
  52.5 24.9 %collective-permute-start.22 = (bf16[32,3584]{1,0:T(8,128)(2,1)S(1)}, bf16[32,3584]{1,0:T(8,128)(2,1)S(1)}, u32[]{:S(2)}, u32[]{:S(2)}) collective-permute-start(bf16[32,3584]{1,0:T(8,128)(2,1)S(1)} %shard_map.92.own_ref), channel_id=1, source_target_pairs={{0,8},{4,12},{8,0},{12,4},{1,9},{5,13},{9,1},{13,5},{2,10},{6,14},... | collective-permute-start | bytes 688136 | tf_op jit(solution)/shard_map/ppermute | solution.py:27
  55.1 17.6 %collective-permute-start.7 = (bf16[32,3584]{1,0:T(8,128)(2,1)S(1)}, bf16[32,3584]{1,0:T(8,128)(2,1)S(1)}, u32[]{:S(2)}, u32[]{:S(2)}) collective-permute-start(bf16[32,3584]{1,0:T(8,128)(2,1)S(1)} %get-tuple-element.20.own_ref), channel_id=1, source_target_pairs={{0,8},{4,12},{8,0},{12,4},{1,9},{5,13},{9,1},{13,5},{2,10},{6,14},... | collective-permute-start | bytes 688136 | tf_op jit(solution)/shard_map/ppermute | solution.py:27
  55.4 17.3 %collective-permute-start.14 = (bf16[32,3584]{1,0:T(8,128)(2,1)S(1)}, bf16[32,3584]{1,0:T(8,128)(2,1)S(1)}, u32[]{:S(2)}, u32[]{:S(2)}) collective-permute-start(bf16[32,3584]{1,0:T(8,128)(2,1)S(1)} %collective-permute-done.13.far_ref), channel_id=1, source_target_pairs={{0,4},{4,0},{8,12},{12,8},{1,5},{5,1},{9,13},{13,9},{2,6},{6,2},{1... | collective-permute-start | bytes 688136 | tf_op jit(solution)/shard_map/ppermute | solution.py:27
  56.8 22.6 %collective-permute-start.17 = (bf16[32,3584]{1,0:T(8,128)(2,1)S(1)}, bf16[32,3584]{1,0:T(8,128)(2,1)S(1)}, u32[]{:S(2)}, u32[]{:S(2)}) collective-permute-start(bf16[32,3584]{1,0:T(8,128)(2,1)S(1)} %collective-permute-done.16.far_ref), channel_id=1, source_target_pairs={{0,4},{4,0},{8,12},{12,8},{1,5},{5,1},{9,13},{13,9},{2,6},{6,2},{1... | collective-permute-start | bytes 688136 | tf_op jit(solution)/shard_map/ppermute | solution.py:27
  72.7 9.6 %collective-permute-start.6 = (bf16[32,3584]{1,0:T(8,128)(2,1)S(1)}, bf16[32,3584]{1,0:T(8,128)(2,1)S(1)}, u32[]{:S(2)}, u32[]{:S(2)}) collective-permute-start(bf16[32,3584]{1,0:T(8,128)(2,1)S(1)} %get-tuple-element.20.own_ref), channel_id=1, source_target_pairs={{0,4},{4,0},{8,12},{12,8},{1,5},{5,1},{9,13},{13,9},{2,6},{6,2},{1... | collective-permute-start | bytes 688136 | tf_op jit(solution)/shard_map/ppermute | solution.py:27
  72.7 14.1 %collective-permute-start.8 = (bf16[32,3584]{1,0:T(8,128)(2,1)S(1)}, bf16[32,3584]{1,0:T(8,128)(2,1)S(1)}, u32[]{:S(2)}, u32[]{:S(2)}) collective-permute-start(bf16[32,3584]{1,0:T(8,128)(2,1)S(1)} %collective-permute-done.7.far_ref), channel_id=1, source_target_pairs={{0,4},{4,0},{8,12},{12,8},{1,5},{5,1},{9,13},{13,9},{2,6},{6,2},{1... | collective-permute-start | bytes 688136 | tf_op jit(solution)/shard_map/ppermute | solution.py:27
  77.2 14.5 %collective-permute-start.21 = (bf16[32,3584]{1,0:T(8,128)(2,1)S(1)}, bf16[32,3584]{1,0:T(8,128)(2,1)S(1)}, u32[]{:S(2)}, u32[]{:S(2)}) collective-permute-start(bf16[32,3584]{1,0:T(8,128)(2,1)S(1)} %shard_map.92.own_ref), channel_id=1, source_target_pairs={{0,4},{4,0},{8,12},{12,8},{1,5},{5,1},{9,13},{13,9},{2,6},{6,2},{1... | collective-permute-start | bytes 688136 | tf_op jit(solution)/shard_map/ppermute | solution.py:27
  77.3 17.8 %collective-permute-start.23 = (bf16[32,3584]{1,0:T(8,128)(2,1)S(1)}, bf16[32,3584]{1,0:T(8,128)(2,1)S(1)}, u32[]{:S(2)}, u32[]{:S(2)}) collective-permute-start(bf16[32,3584]{1,0:T(8,128)(2,1)S(1)} %collective-permute-done.22.far_ref), channel_id=1, source_target_pairs={{0,4},{4,0},{8,12},{12,8},{1,5},{5,1},{9,13},{13,9},{2,6},{6,2},{1... | collective-permute-start | bytes 688136 | tf_op jit(solution)/shard_map/ppermute | solution.py:27
  79.3 18.9 %collective-permute-start.19 = (bf16[64,1792]{1,0:T(8,128)(2,1)S(1)}, bf16[64,1792]{1,0:T(8,128)(2,1)S(1)}, u32[]{:S(2)}, u32[]{:S(2)}) collective-permute-start(bf16[64,1792]{1,0:T(8,128)(2,1)S(1)} %get-tuple-element.27), channel_id=1, source_target_pairs={{0,2},{2,0},{1,3},{3,1},{4,6},{6,4},{5,7},{7,5},{8,10},{10,8},{9,1... | collective-permute-start | bytes 688136 | tf_op jit(solution)/shard_map/ppermute | solution.py:27
  82.3 15.9 %collective-permute-start.20 = (bf16[64,1792]{1,0:T(8,128)(2,1)S(1)}, bf16[64,1792]{1,0:T(8,128)(2,1)S(1)}, u32[]{:S(2)}, u32[]{:S(2)}) collective-permute-start(bf16[64,1792]{1,0:T(8,128)(2,1)S(1)} %get-tuple-element.28), channel_id=1, source_target_pairs={{0,2},{2,0},{1,3},{3,1},{4,6},{6,4},{5,7},{7,5},{8,10},{10,8},{9,1... | collective-permute-start | bytes 688136 | tf_op jit(solution)/shard_map/ppermute | solution.py:27
  89.3 9.0 %collective-permute-start.18 = (bf16[64,1792]{1,0:T(8,128)(2,1)S(1)}, bf16[64,1792]{1,0:T(8,128)(2,1)S(1)}, u32[]{:S(2)}, u32[]{:S(2)}) collective-permute-start(bf16[64,1792]{1,0:T(8,128)(2,1)S(1)} %get-tuple-element.26), channel_id=1, source_target_pairs={{0,2},{2,0},{1,3},{3,1},{4,6},{6,4},{5,7},{7,5},{8,10},{10,8},{9,1... | collective-permute-start | bytes 688136 | tf_op jit(solution)/shard_map/ppermute | solution.py:27
  97.6 6.1 %collective-permute-start.24 = (bf16[64,1792]{1,0:T(8,128)(2,1)S(1)}, bf16[64,1792]{1,0:T(8,128)(2,1)S(1)}, u32[]{:S(2)}, u32[]{:S(2)}) collective-permute-start(bf16[64,1792]{1,0:T(8,128)(2,1)S(1)} %get-tuple-element.30), channel_id=1, source_target_pairs={{0,2},{2,0},{1,3},{3,1},{4,6},{6,4},{5,7},{7,5},{8,10},{10,8},{9,1... | collective-permute-start | bytes 688136 | tf_op jit(solution)/shard_map/ppermute | solution.py:27
  (10 other events, 200.5 us)
